TPU v7x, 256 devices: a whole 4x4x8 slice. The times are simulated.
256 devices in a mesh: view: 16 (over x, z_lo), slab: 16 (over z_hi, y, core).
Axes of the slice: x: 4, y: 4, z: 8 (z_hi: 2, z_lo: 4; z = z_hi * 4 + z_lo), core: 2. Of those that a mesh axis runs over, the one named last changes fastest.
Arguments:
- estimate: float32 [256, 64, 512], P('slab', 'view'), may hold values from 0.5 to 2
- observed: float32 [16, 256, 64, 512], P('view', 'slab'), may hold values from 0.5 to 2
- psf_z: float32 [16, 3, 31], P('view'), may hold values from 0.01 to 1
- psf_y: float32 [16, 3, 31], P('view'), may hold values from 0.01 to 1
- psf_x: float32 [16, 3, 31], P('view'), may hold values from 0.01 to 1
Outputs:
- updated: float32 [256, 64, 512], P('slab', 'view')
All inputs are finite; a program needn't handle non-finite values.
Results may differ from a plain program's by a relative error of at most 0.00018.
Values sent between devices are 32-bit elements; how exact they have to be, the bound alone decides.
A program may use at most 128 MiB of HBM per device.

v0:
```python
import jax
import jax.numpy as jnp
from jax import lax
from jax.sharding import PartitionSpec as P

RANK = 3
TAPS = 31
HALF = 15


def extended(shard, sides, width):
    for axis, dim in sides:
        peers, length = (lax.axis_size(axis), shard.shape[dim])
        up = [(i, (i + 1) % peers) for i in range(peers - 1)]
        down = [(j, i) for i, j in up]
        last = lax.slice_in_dim(shard, length - width, length, axis=dim)
        first = lax.slice_in_dim(shard, 0, width, axis=dim)
        before = lax.ppermute(last, axis, up)
        after = lax.ppermute(first, axis, down)
        shard = jnp.concatenate([before, shard, after], axis=dim)
    return shard


def in_order(blocks, dim):
    blocks = jnp.moveaxis(blocks, 0, dim)
    shape = blocks.shape
    return blocks.reshape(*shape[:dim], shape[dim] * shape[dim + 1], *shape[dim + 2 :])


def from_everyone(shard, axis):
    copies = jnp.broadcast_to(shard, (lax.axis_size(axis), *shard.shape))
    return lax.all_to_all(copies, axis, split_axis=0, concat_axis=0, tiled=True)


def collect(shard, axis, dim):
    return in_order(from_everyone(shard, axis), dim)


def cut_along(shard, dim, peers):
    before, after = (shard.shape[:dim], shard.shape[dim + 1 :])
    return jnp.moveaxis(shard.reshape(*before, peers, -1, *after), dim, 0)


def sent_and_summed(shard, axis, dim):
    peers = lax.axis_size(axis)
    blocks = lax.all_to_all(cut_along(shard, dim, peers), axis, 0, 0, tiled=True)
    return jnp.sum(blocks, axis=0)


def band_table(taps, count_rows, count_cols, offset):
    rows = jnp.arange(count_rows, dtype=jnp.int32)[:, None]
    cols = jnp.arange(count_cols, dtype=jnp.int32)[None, :]
    spread = cols - rows + offset
    table = jnp.zeros((taps.shape[0], count_rows, count_cols), jnp.float32)
    for k in range(TAPS):
        table = table + taps[:, k][:, None, None] * (spread == k).astype(jnp.float32)[None]
    return table


def block_tables(taps, block_size):
    full = band_table(taps, block_size, block_size + 2 * HALF, 0)
    centre = full[:, :, HALF : HALF + block_size]
    edges = jnp.concatenate([full[:, :, :HALF], full[:, :, HALF + block_size :]], 2)
    return (centre, edges)


def x_blur(volume, centre, edges):
    high = lax.Precision.HIGHEST
    depth, height, width = volume.shape
    block_size = centre.shape[0]
    block_count = width // block_size
    blocks = volume.reshape(depth, height, block_count, block_size)
    zero_edge = jnp.zeros((depth, height, 1, HALF), volume.dtype)
    left_rim = jnp.concatenate([zero_edge, blocks[:, :, : block_count - 1, block_size - HALF :]], 2)
    right_rim = jnp.concatenate([blocks[:, :, 1:, :HALF], zero_edge], 2)
    both_rims = jnp.concatenate([left_rim, right_rim], 3)
    result = jnp.einsum("zynj,ij->zyni", blocks, centre, precision=high)
    result = result + jnp.einsum("zynj,ij->zyni", both_rims, edges, precision=high)
    return result.reshape(depth, height, width)


def view_log(field, seen, taps_z, taps_y, taps_x):
    high = lax.Precision.HIGHEST
    depth, height, width = field.shape
    block_size = min(128, width)
    centre, edges = block_tables(taps_x, block_size)
    centre_back, edges_back = block_tables(taps_x[:, ::-1], block_size)
    mat_y = band_table(taps_y, height, height, HALF)
    mat_z = band_table(taps_z, depth, depth + 2 * HALF, 0)
    mat_zt = band_table(taps_z[:, ::-1], depth, depth + 2 * HALF, 0)
    empty = jnp.zeros_like(field)
    padded = extended(field, (("slab", 0),), HALF)

    def forward(r, total):
        part = jnp.einsum("ip,pyx->iyx", mat_z[r], padded, precision=high)
        part = x_blur(part, centre[r], edges[r])
        return total + jnp.einsum("zjx,ij->zix", part, mat_y[r], precision=high)

    blurred = lax.fori_loop(0, RANK, forward, empty)
    ratio = seen / blurred
    ratio_pad = extended(ratio, (("slab", 0),), HALF)

    def backward(r, total):
        part = jnp.einsum("jp,pyx->jyx", mat_zt[r], ratio_pad, precision=high)
        part = x_blur(part, centre_back[r], edges_back[r])
        return total + jnp.einsum("zix,ij->zjx", part, mat_y[r], precision=high)

    back = lax.fori_loop(0, RANK, backward, empty)
    return jnp.log(back)


def local(estimate, observed, psf_z, psf_y, psf_x):
    gathered = collect(estimate, "view", 1)
    logsum = view_log(gathered, observed[0], psf_z[0], psf_y[0], psf_x[0])
    share = sent_and_summed(logsum, "view", 1)
    owned = estimate * jnp.exp(share)
    return owned


def solution(mesh):
    placed = (
        P("slab", "view", None),
        P("view", "slab", None, None),
        P("view", None, None),
        P("view", None, None),
        P("view", None, None),
    )
    return jax.shard_map(
        local, mesh=mesh, in_specs=placed, out_specs=P("slab", "view", None), check_vma=False
    )
```

profile of v0, /device:TPU:25, one launch (start us, length us, event | category | flops | bytes accessed | tf_op | source)
XLA Modules:
  0.0 389.4 jit_solution(9201551562441473698)
XLA Ops:
  2.6 8.4 %all-to-all-start = ((f32[16,16,4,512]{3,2,1,0:T(4,128)}), f32[16,16,4,512]{3,2,1,0:T(4,128)}, u32[]{:S(2)}, u32[]{:S(2)}) async-start(f32[16,16,4,512]{3,2,1,0:T(4,128)} %broadcast_in_dim.5), calls=%async_computation | async-start | bytes 4194304 | tf_op jit(solution)/shard_map/all_to_all | solution.py:32
  31.6 29.3 %all-to-all-done = f32[16,16,4,512]{3,2,1,0:T(4,128)} async-done(((f32[16,16,4,512]{3,2,1,0:T(4,128)}), f32[16,16,4,512]{3,2,1,0:T(4,128)}, u32[]{:S(2)}, u32[]{:S(2)}) %all-to-all-start) | async-done | bytes 2097184 | tf_op jit(solution)/shard_map/all_to_all | solution.py:32
  69.7 8.5 %collective-permute-start = (f32[15,64,512]{2,1,0:T(8,128)S(1)}, f32[15,64,512]{2,1,0:T(8,128)S(1)}, u32[]{:S(2)}, u32[]{:S(2)}) collective-permute-start(f32[15,64,512]{2,1,0:T(8,128)S(1)} %copy.112), channel_id=1, source_target_pairs={{0,1},{1,2},{2,3},{3,4},{4,5},{5,6},{6,7},{7,8},{8,9},{9,10},{10,1... | collective-permute-start | bytes 5898248 | tf_op jit(solution)/shard_map/ppermute | solution.py:18
  81.7 16.8 %collective-permute-done.1 = f32[15,64,512]{2,1,0:T(8,128)S(1)} collective-permute-done((f32[15,64,512]{2,1,0:T(8,128)S(1)}, f32[15,64,512]{2,1,0:T(8,128)S(1)}, u32[]{:S(2)}, u32[]{:S(2)}) %collective-permute-start.1) | collective-permute-done | bytes 1966112 | tf_op jit(solution)/shard_map/ppermute | solution.py:19
  101.9 6.1 %copy.101 = f32[46,64,512]{2,1,0:T(8,128)} copy(f32[46,64,512]{2,0,1:T(8,128)S(1)} %pad_maximum_fusion) | data formatting | bytes 12058624
  108.0 84.5 %while.28 = (s32[]{:T(128)}, f32[16,64,512]{2,1,0:T(8,128)S(1)}, f32[3,64,64]{1,2,0:T(8,128)S(1)}, f32[3,16,46]{2,1,0:T(8,128)}, f32[46,64,512]{2,1,0:T(8,128)},...) while((s32[]{:T(128)}, f32[16,64,512]{2,1,0:T(8,128)S(1)}, ...), condition=%wide.region_1.0_spmd.clone, body=%wide.region_0.0_spmd.clone.sunk | while | flops 1688297472 | bytes 37077116 | solution.py:99
  108.4 7.5 %dot_general.74 = f32[64,4,128,46]{2,1,0,3:T(4,128)} reshape(f32[64,512,46]{1,0,2:T(8,128)} %bitcast.133) | data formatting | bytes 12058624 | tf_op jit(solution)/shard_map/while/body/eval_jaxpr/ip,pyx->iyx/dot_general | solution.py:95
  115.9 9.5 %fusion.333 = f32[16,64,4,128]{3,0,2,1:T(8,128)S(1)} fusion(f32[64,4,128,46]{2,1,0,3:T(4,128)} %dot_general.74, f32[3,16,46]{2,1,0:T(8,128)} %get-tuple-element.727, s32[]{:T(128)S(6)} %copy.178), kind=kOutput, calls=%fused_computation.clone.1 | convolution fusion | flops 289406976 | bytes 8134660 | tf_op jit(solution)/shard_map/while/body/eval_jaxpr/ip,pyx->iyx/dot_general | solution.py:95
  136.3 7.5 %dot_general.74 = f32[64,4,128,46]{2,1,0,3:T(4,128)} reshape(f32[64,512,46]{1,0,2:T(8,128)} %bitcast.133) | data formatting | bytes 12058624 | tf_op jit(solution)/shard_map/while/body/eval_jaxpr/ip,pyx->iyx/dot_general | solution.py:95
  143.8 9.5 %fusion.333 = f32[16,64,4,128]{3,0,2,1:T(8,128)S(1)} fusion(f32[64,4,128,46]{2,1,0,3:T(4,128)} %dot_general.74, f32[3,16,46]{2,1,0:T(8,128)} %get-tuple-element.727, s32[]{:T(128)S(6)} %copy.178), kind=kOutput, calls=%fused_computation.clone.1 | convolution fusion | flops 289406976 | bytes 8134660 | tf_op jit(solution)/shard_map/while/body/eval_jaxpr/ip,pyx->iyx/dot_general | solution.py:95
  164.3 7.5 %dot_general.74 = f32[64,4,128,46]{2,1,0,3:T(4,128)} reshape(f32[64,512,46]{1,0,2:T(8,128)} %bitcast.133) | data formatting | bytes 12058624 | tf_op jit(solution)/shard_map/while/body/eval_jaxpr/ip,pyx->iyx/dot_general | solution.py:95
  171.8 9.5 %fusion.333 = f32[16,64,4,128]{3,0,2,1:T(8,128)S(1)} fusion(f32[64,4,128,46]{2,1,0,3:T(4,128)} %dot_general.74, f32[3,16,46]{2,1,0:T(8,128)} %get-tuple-element.727, s32[]{:T(128)S(6)} %copy.178), kind=kOutput, calls=%fused_computation.clone.1 | convolution fusion | flops 289406976 | bytes 8134660 | tf_op jit(solution)/shard_map/while/body/eval_jaxpr/ip,pyx->iyx/dot_general | solution.py:95
  197.1 10.4 %collective-permute-start.2 = (f32[15,64,512]{2,1,0:T(8,128)}, f32[15,64,512]{2,1,0:T(8,128)}, u32[]{:S(2)}, u32[]{:S(2)}) collective-permute-start(f32[15,64,512]{2,1,0:T(8,128)} %get-tuple-element.512), channel_id=1, source_target_pairs={{0,1},{1,2},{2,3},{3,4},{4,5},{5,6},{6,7},{7,8},{8,9},{9,10},{10,1... | collective-permute-start | bytes 5898248 | tf_op jit(solution)/shard_map/ppermute | solution.py:18
  213.2 16.2 %collective-permute-done.2 = f32[15,64,512]{2,1,0:T(8,128)} collective-permute-done((f32[15,64,512]{2,1,0:T(8,128)}, f32[15,64,512]{2,1,0:T(8,128)}, u32[]{:S(2)}, u32[]{:S(2)}) %collective-permute-start.2) | collective-permute-done | bytes 1966112 | tf_op jit(solution)/shard_map/ppermute | solution.py:18
  229.4 10.5 %collective-permute-done.3 = f32[15,64,512]{2,1,0:T(8,128)} collective-permute-done((f32[15,64,512]{2,1,0:T(8,128)}, f32[15,64,512]{2,1,0:T(8,128)}, u32[]{:S(2)}, u32[]{:S(2)}) %collective-permute-start.3) | collective-permute-done | bytes 1966112 | tf_op jit(solution)/shard_map/ppermute | solution.py:19
  239.9 5.7 %pad_maximum_fusion.1 = f32[46,64,512]{2,1,0:T(8,128)} fusion(f32[15,64,512]{2,1,0:T(8,128)} %collective-permute-done.3, f32[16,64,512]{2,1,0:T(8,128)S(1)} %copy-done.1, f32[15,64,512]{2,1,0:T(8,128)} %collective-permute-done.2), kind=kLoop, calls=%fused_computation.53 | loop fusion | flops 3014656 | bytes 12058624 | tf_op jit(solution)/shard_map/concatenate | solution.py:20
  245.6 81.8 %while.29 = (s32[]{:T(128)}, f32[16,64,512]{2,1,0:T(8,128)S(1)}, f32[3,64,64]{1,2,0:T(8,128)S(1)}, f32[3,16,46]{2,1,0:T(8,128)S(1)}, f32[46,64,512]{2,1,0:T(8,12...) while((s32[]{:T(128)}, f32[16,64,512]{2,1,0:T(8,128)S(1)}, ...), condition=%wide.region_3.0_spmd.clone, body=%wide.region_2.0_spmd.clone.sunk | while | flops 1688297472 | bytes 38682748 | solution.py:108
  245.6 7.5 %dot_general.75 = f32[64,4,128,46]{2,1,0,3:T(4,128)} reshape(f32[64,512,46]{1,0,2:T(8,128)} %bitcast.132) | data formatting | bytes 12058624 | tf_op jit(solution)/shard_map/while/body/eval_jaxpr/jp,pyx->jyx/dot_general | solution.py:104
  253.0 9.4 %fusion.344 = f32[16,64,4,128]{3,0,2,1:T(8,128)S(1)} fusion(f32[64,4,128,46]{2,1,0,3:T(4,128)} %dot_general.75, f32[3,16,46]{2,1,0:T(8,128)S(1)} %get-tuple-element.754, s32[]{:T(128)S(6)} %copy.184), kind=kOutput, calls=%fused_computation.26.clone.1 | convolution fusion | flops 289406976 | bytes 8134660 | tf_op jit(solution)/shard_map/while/body/eval_jaxpr/jp,pyx->jyx/dot_general | solution.py:104
  272.7 7.5 %dot_general.75 = f32[64,4,128,46]{2,1,0,3:T(4,128)} reshape(f32[64,512,46]{1,0,2:T(8,128)} %bitcast.132) | data formatting | bytes 12058624 | tf_op jit(solution)/shard_map/while/body/eval_jaxpr/jp,pyx->jyx/dot_general | solution.py:104
  280.2 9.4 %fusion.344 = f32[16,64,4,128]{3,0,2,1:T(8,128)S(1)} fusion(f32[64,4,128,46]{2,1,0,3:T(4,128)} %dot_general.75, f32[3,16,46]{2,1,0:T(8,128)S(1)} %get-tuple-element.754, s32[]{:T(128)S(6)} %copy.184), kind=kOutput, calls=%fused_computation.26.clone.1 | convolution fusion | flops 289406976 | bytes 8134660 | tf_op jit(solution)/shard_map/while/body/eval_jaxpr/jp,pyx->jyx/dot_general | solution.py:104
  299.9 7.5 %dot_general.75 = f32[64,4,128,46]{2,1,0,3:T(4,128)} reshape(f32[64,512,46]{1,0,2:T(8,128)} %bitcast.132) | data formatting | bytes 12058624 | tf_op jit(solution)/shard_map/while/body/eval_jaxpr/jp,pyx->jyx/dot_general | solution.py:104
  307.4 9.4 %fusion.344 = f32[16,64,4,128]{3,0,2,1:T(8,128)S(1)} fusion(f32[64,4,128,46]{2,1,0,3:T(4,128)} %dot_general.75, f32[3,16,46]{2,1,0:T(8,128)S(1)} %get-tuple-element.754, s32[]{:T(128)S(6)} %copy.184), kind=kOutput, calls=%fused_computation.26.clone.1 | convolution fusion | flops 289406976 | bytes 8134660 | tf_op jit(solution)/shard_map/while/body/eval_jaxpr/jp,pyx->jyx/dot_general | solution.py:104
  330.1 57.4 %all_to_all.10 = f32[16,16,4,512]{3,2,1,0:T(4,128)S(1)} all-to-all(f32[16,16,4,512]{3,2,1,0:T(4,128)S(1)} %copy.105), channel_id=1, replica_groups=mesh['view'=16,'slab'=16] {'view'}, dimensions={0} | all-to-all | bytes 4194304 | tf_op jit(solution)/shard_map/all_to_all | solution.py:46
  (301 shorter events, 115.6 us)
Async XLA Ops:
  2.6 58.3 %all-to-all-start = ((f32[16,16,4,512]{3,2,1,0:T(4,128)}), f32[16,16,4,512]{3,2,1,0:T(4,128)}, u32[]{:S(2)}, u32[]{:S(2)}) async-start(f32[16,16,4,512]{3,2,1,0:T(4,128)} %broadcast_in_dim.5), calls=%async_computation | async-start | bytes 4194304 | tf_op jit(solution)/shard_map/all_to_all | solution.py:32
  17.6 60.8 %copy-start.27 = (f32[16,46]{1,0:T(8,128)}, f32[16,46]{1,0:T(8,128)S(1)}, u32[]{:S(2)}) copy-start(f32[16,46]{1,0:T(8,128)S(1)} %get-tuple-element.608) | copy-start | bytes 8836
  17.6 60.8 %copy-start.28 = (f32[16,46]{1,0:T(8,128)}, f32[16,46]{1,0:T(8,128)S(1)}, u32[]{:S(2)}) copy-start(f32[16,46]{1,0:T(8,128)S(1)} %get-tuple-element.609) | copy-start | bytes 8836
  17.7 60.8 %copy-start.29 = (f32[16,46]{1,0:T(8,128)}, f32[16,46]{1,0:T(8,128)S(1)}, u32[]{:S(2)}) copy-start(f32[16,46]{1,0:T(8,128)S(1)} %get-tuple-element.606) | copy-start | bytes 8836
  17.7 60.8 %copy-start.30 = (f32[16,46]{1,0:T(8,128)}, f32[16,46]{1,0:T(8,128)S(1)}, u32[]{:S(2)}) copy-start(f32[16,46]{1,0:T(8,128)S(1)} %get-tuple-element.607) | copy-start | bytes 8836
  17.7 60.7 %copy-start.31 = (f32[16,46]{1,0:T(8,128)}, f32[16,46]{1,0:T(8,128)S(1)}, u32[]{:S(2)}) copy-start(f32[16,46]{1,0:T(8,128)S(1)} %get-tuple-element.604) | copy-start | bytes 8836
  17.7 60.7 %copy-start.32 = (f32[16,46]{1,0:T(8,128)}, f32[16,46]{1,0:T(8,128)S(1)}, u32[]{:S(2)}) copy-start(f32[16,46]{1,0:T(8,128)S(1)} %get-tuple-element.605) | copy-start | bytes 8836
  65.2 15.3 %copy-start.20 = (f32[64,64]{0,1:T(8,128)S(1)}, f32[64,64]{0,1:T(8,128)}, u32[]{:S(2)}) copy-start(f32[64,64]{0,1:T(8,128)} %fusion.203) | copy-start | bytes 49156
  65.2 15.3 %copy-start.21 = (f32[64,64]{0,1:T(8,128)S(1)}, f32[64,64]{0,1:T(8,128)}, u32[]{:S(2)}) copy-start(f32[64,64]{0,1:T(8,128)} %get-tuple-element.580) | copy-start | bytes 49156
  65.2 15.3 %copy-start.22 = (f32[64,64]{0,1:T(8,128)S(1)}, f32[64,64]{0,1:T(8,128)}, u32[]{:S(2)}) copy-start(f32[64,64]{0,1:T(8,128)} %get-tuple-element.581) | copy-start | bytes 49156
  65.2 15.3 %copy-start.23 = (f32[64,64]{0,1:T(8,128)S(1)}, f32[64,64]{0,1:T(8,128)}, u32[]{:S(2)}) copy-start(f32[64,64]{0,1:T(8,128)} %get-tuple-element.578) | copy-start | bytes 49156
  65.2 15.3 %copy-start.24 = (f32[64,64]{0,1:T(8,128)S(1)}, f32[64,64]{0,1:T(8,128)}, u32[]{:S(2)}) copy-start(f32[64,64]{0,1:T(8,128)} %get-tuple-element.579) | copy-start | bytes 49156
  65.2 15.3 %copy-start.25 = (f32[64,64]{0,1:T(8,128)S(1)}, f32[64,64]{0,1:T(8,128)}, u32[]{:S(2)}) copy-start(f32[64,64]{0,1:T(8,128)} %get-tuple-element.576) | copy-start | bytes 49156
  65.2 15.3 %copy-start.26 = (f32[64,64]{0,1:T(8,128)S(1)}, f32[64,64]{0,1:T(8,128)}, u32[]{:S(2)}) copy-start(f32[64,64]{0,1:T(8,128)} %get-tuple-element.577) | copy-start | bytes 49156
  66.4 32.1 %collective-permute-start.1 = (f32[15,64,512]{2,1,0:T(8,128)S(1)}, f32[15,64,512]{2,1,0:T(8,128)S(1)}, u32[]{:S(2)}, u32[]{:S(2)}) collective-permute-start(f32[15,64,512]{2,1,0:T(8,128)S(1)} %copy.113), channel_id=1, source_target_pairs={{1,0},{2,1},{3,2},{4,3},{5,4},{6,5},{7,6},{8,7},{9,8},{10,9},{11,1... | collective-permute-start | bytes 5898248 | tf_op jit(solution)/shard_map/ppermute | solution.py:19
  69.7 29.9 %collective-permute-start = (f32[15,64,512]{2,1,0:T(8,128)S(1)}, f32[15,64,512]{2,1,0:T(8,128)S(1)}, u32[]{:S(2)}, u32[]{:S(2)}) collective-permute-start(f32[15,64,512]{2,1,0:T(8,128)S(1)} %copy.112), channel_id=1, source_target_pairs={{0,1},{1,2},{2,3},{3,4},{4,5},{5,6},{6,7},{7,8},{8,9},{9,10},{10,1... | collective-permute-start | bytes 5898248 | tf_op jit(solution)/shard_map/ppermute | solution.py:18
  78.2 21.4 %copy-start.55 = (f32[16,46]{1,0:T(8,128)}, f32[16,46]{1,0:T(8,128)S(1)}, u32[]{:S(2)}) copy-start(f32[16,46]{1,0:T(8,128)S(1)} %fusion.295) | copy-start | bytes 8836
  194.5 14.9 %copy-start.3 = (f32[128,158]{0,1:T(8,128)S(1)}, f32[128,158]{0,1:T(8,128)}, u32[]{:S(2)}) copy-start(f32[128,158]{0,1:T(8,128)} %copy-done.2) | copy-start | bytes 242692
  194.5 14.9 %copy-start.5 = (f32[128,158]{0,1:T(8,128)S(1)}, f32[128,158]{0,1:T(8,128)}, u32[]{:S(2)}) copy-start(f32[128,158]{0,1:T(8,128)} %copy-done.4) | copy-start | bytes 242692
  194.6 14.9 %copy-start.57 = (f32[3]{0:T(128)S(1)}, f32[3]{0:T(128)}, u32[]{:S(2)}) copy-start(f32[3]{0:T(128)} %copy-done.56) | copy-start | bytes 40
  194.6 14.9 %copy-start.59 = (f32[3]{0:T(128)S(1)}, f32[3]{0:T(128)}, u32[]{:S(2)}) copy-start(f32[3]{0:T(128)} %copy-done.58) | copy-start | bytes 40
  197.1 32.3 %collective-permute-start.2 = (f32[15,64,512]{2,1,0:T(8,128)}, f32[15,64,512]{2,1,0:T(8,128)}, u32[]{:S(2)}, u32[]{:S(2)}) collective-permute-start(f32[15,64,512]{2,1,0:T(8,128)} %get-tuple-element.512), channel_id=1, source_target_pairs={{0,1},{1,2},{2,3},{3,4},{4,5},{5,6},{6,7},{7,8},{8,9},{9,10},{10,1... | collective-permute-start | bytes 5898248 | tf_op jit(solution)/shard_map/ppermute | solution.py:18
  207.5 32.4 %collective-permute-start.3 = (f32[15,64,512]{2,1,0:T(8,128)}, f32[15,64,512]{2,1,0:T(8,128)}, u32[]{:S(2)}, u32[]{:S(2)}) collective-permute-start(f32[15,64,512]{2,1,0:T(8,128)} %get-tuple-element.513), channel_id=1, source_target_pairs={{1,0},{2,1},{3,2},{4,3},{5,4},{6,5},{7,6},{8,7},{9,8},{10,9},{11,1... | collective-permute-start | bytes 5898248 | tf_op jit(solution)/shard_map/ppermute | solution.py:19
  209.5 30.3 %copy-start.1 = (f32[16,64,512]{2,1,0:T(8,128)S(1)}, f32[16,64,512]{2,1,0:T(8,128)}, u32[]{:S(2)}) copy-start(f32[16,64,512]{2,1,0:T(8,128)} %copy-done) | copy-start | bytes 6291460
  (73 other events, 719.4 us)
where the time goes:
time: 397 us; the launch traced here: 389 us
  matrix products  114 us (29%)
  local copies, waits for them, and re-layouts  77.7 us (20%)
  waiting for transfers between devices  72.7 us (18%)
  blocking collectives  57.4 us (14%)
  starting transfers between devices  32.4 us (8%)
  other arithmetic  31.9 us (8%)
    all_to_all x1, blocking collectives, sent_and_summed(): lax.all_to_all(cut_along(shard, dim, peers), axis, 0, 0, tiled=True)  57.4 us
    all_to_all x1, waiting for transfers between devices, from_everyone(): return lax.all_to_all(copies, axis, split_axis=0, concat_axis=0, tiled=True)  29.3 us
    dot_general x3, matrix products, forward(): part = jnp.einsum('ip,pyx->iyx', mat_z[r], padded, precision=high)  28.4 us
    dot_general x3, matrix products, backward(): part = jnp.einsum('jp,pyx->jyx', mat_zt[r], ratio_pad, precision=high)  28.3 us
    ppermute x2, waiting for transfers between devices, extended(): after = lax.ppermute(first, axis, down)  27.3 us
    dot_general x6, matrix products, x_blur(): jnp.einsum('zynj,ij->zyni', both_rims, edges, precision=high)  22.5 us
    dot_general x3, local copies, waits for them, and re-layouts, forward(): part = jnp.einsum('ip,pyx->iyx', mat_z[r], padded, precision=high)  22.5 us
    dot_general x3, local copies, waits for them, and re-layouts, backward(): part = jnp.einsum('jp,pyx->jyx', mat_zt[r], ratio_pad, precision=high)  22.5 us
  transfers between devices with their start and end apart: 5, of which 4 were waited for; matrix products, arithmetic and copies ran while one was open for 7% of the time, Pallas kernels for 0%

commit v1 on v0

v1 whole, which is shorter than its diff:
```python
import functools

import jax
import jax.numpy as jnp
from jax import lax
from jax.experimental import pallas as pl
from jax.experimental.pallas import tpu as pltpu
from jax.sharding import PartitionSpec as P

RANK = 3
TAPS = 31
HALF = 15
F32, BF16 = jnp.float32, jnp.bfloat16


def split(x):
    hi = x.astype(BF16)
    return hi, (x - hi.astype(F32)).astype(BF16)


def pick(code, count, tap):
    def one(k, acc):
        return jnp.where(code == k, tap(k), acc)

    return lax.fori_loop(0, count, one, jnp.zeros(code.shape, F32))


def iotas(shape):
    return [lax.broadcasted_iota(jnp.int32, shape, d) for d in range(2)]


def build_tables(pz, py, px, wz, wy, cx, ex, back):
    def tap_of(ref):
        return lambda k: ref[k // 32, k % 32]

    row, col = iotas((48, 96))
    p = jnp.where(col < 48, col, col - 48)
    d = (row % 16) - p + 31 if back else p - (row % 16) - 1
    code = jnp.where((d >= 0) & (d < TAPS), (row // 16) * 32 + d, -1)
    hi, lo = split(pick(code, RANK * 32, tap_of(pz)))
    wz[0:48, :] = hi
    wz[48:96, :] = jnp.where(col < 48, lo.astype(F32), 0.0).astype(BF16)

    row, col = iotas((64, 384))
    c = jnp.where(col < 192, col, col - 192)
    d = row - (c % 64) + HALF if back else (c % 64) - row + HALF
    code = jnp.where((d >= 0) & (d < TAPS), (c // 64) * 32 + d, -1)
    hi, lo = split(pick(code, RANK * 32, tap_of(py)))
    wy[0:64, :] = hi
    wy[64:128, :] = jnp.where(col < 192, lo.astype(F32), 0.0).astype(BF16)

    row, col = iotas((128, 128))
    d = col - row + HALF if back else row - col + HALF
    ring = lax.rem(d + 128, 128)
    near = (d >= 0) & (d < TAPS)
    zero = jnp.zeros((128, 128), BF16)
    for r in range(RANK):
        full = pick(ring, TAPS, lambda k: px[r, k])
        for ref, keep in ((cx, near), (ex, jnp.logical_not(near))):
            hi, lo = split(jnp.where(keep, full, 0.0))
            ref[r, 0:128, 0:128] = hi
            ref[r, 0:128, 128:256] = lo
            ref[r, 128:256, 0:128] = hi
            ref[r, 128:256, 128:256] = zero


def dot(a, b):
    return jnp.dot(a, b, preferred_element_type=F32)


def z_stage(src, wz, thi, tlo, unroll=4):
    def one(y, _):
        hi, lo = split(src[y])
        o = dot(wz[...], jnp.concatenate([hi, lo], axis=0))
        hi, lo = split(o[:48] + o[48:])
        thi[y] = hi
        tlo[y] = lo
        return 0

    lax.fori_loop(0, 64, one, 0, unroll=unroll)


def x_stage(thi, tlo, cx, ex, xo, rows=8):
    m = rows * 16
    low = lax.broadcasted_iota(jnp.int32, (m, 128), 1) < 64

    for r in range(RANK):

        def one(c, _):
            ys = pl.ds(c * rows, rows)
            hi = thi[ys, 16 * r : 16 * r + 16, :].reshape(m, 512)
            lo = tlo[ys, 16 * r : 16 * r + 16, :].reshape(m, 512)
            h = [hi[:, 128 * b : 128 * b + 128] for b in range(4)]
            l = [lo[:, 128 * b : 128 * b + 128] for b in range(4)]
            out = []
            for b in range(4):
                o = dot(jnp.concatenate([h[b], l[b]], axis=1), cx[r])
                out.append(o[:, :128] + o[:, 128:])
            for b in range(3):
                ph = jnp.where(low, h[b + 1], h[b])
                pll = jnp.where(low, l[b + 1], l[b])
                o = dot(jnp.concatenate([ph, pll], axis=1), ex[r])
                e = o[:, :128] + o[:, 128:]
                out[b] = out[b] + jnp.where(low, 0.0, e)
                out[b + 1] = out[b + 1] + jnp.where(low, e, 0.0)
            rr = pl.ds(r * 1024 + c * m, m)
            for b in range(4):
                xo[b, rr, :] = out[b]
            return 0

        lax.fori_loop(0, 64 // rows, one, 0)


def y_stage(xo, wy, finish, lo=0, hi=16):
    def one(z, _):
        planes = []
        for r in range(RANK):
            parts = [xo[b, pl.ds(r * 1024 + z, 64, stride=16), :] for b in range(4)]
            planes.append(jnp.concatenate(parts, axis=1))
        h, l = split(jnp.concatenate(planes, axis=0))
        o = dot(wy[...], jnp.concatenate([h, l], axis=0))
        finish(z, o[:64] + o[64:])
        return 0

    lax.fori_loop(lo, hi, one, 0)


TABLES = [
    pltpu.VMEM((96, 96), BF16),
    pltpu.VMEM((128, 384), BF16),
    pltpu.VMEM((3, 256, 256), BF16),
    pltpu.VMEM((3, 256, 256), BF16),
]
WORK = [
    pltpu.VMEM((64, 48, 512), BF16),
    pltpu.VMEM((64, 48, 512), BF16),
    pltpu.VMEM((4, 3072, 128), F32),
]


def forward_kernel(pz, py, px, fld, obs, out, wz, wy, cx, ex, thi, tlo, xo, rat):
    build_tables(pz, py, px, wz, wy, cx, ex, False)
    z_stage(fld, wz, thi, tlo)
    x_stage(thi, tlo, cx, ex, xo)

    def finish(z, blurred):
        ratio = obs[z] / blurred
        for b in range(4):
            rat[b, pl.ds(z, 64, stride=16), :] = ratio[:, 128 * b : 128 * b + 128]

    y_stage(xo, wy, finish)
    for b in range(4):
        out[:, :, 128 * b : 128 * b + 128] = rat[b].reshape(64, 16, 128)


def backward_kernel(pz, py, px, rat, out, wz, wy, cx, ex, thi, tlo, xo):
    build_tables(pz, py, px, wz, wy, cx, ex, True)
    z_stage(rat, wz, thi, tlo)
    x_stage(thi, tlo, cx, ex, xo)

    def finish(z, back):
        out[z] = jnp.log(back)

    y_stage(xo, wy, finish)


SMEM = pl.BlockSpec(memory_space=pltpu.SMEM)
VM = pl.BlockSpec(memory_space=pltpu.VMEM)
PARAMS = dict(vmem_limit_bytes=60 << 20)


def forward(pz, py, px, fld, obs):
    return pl.pallas_call(
        forward_kernel,
        out_shape=jax.ShapeDtypeStruct((64, 16, 512), F32),
        in_specs=[SMEM] * 3 + [VM] * 2,
        out_specs=VM,
        scratch_shapes=TABLES + WORK + [pltpu.VMEM((4, 1024, 128), F32)],
        compiler_params=pltpu.CompilerParams(**PARAMS),
        name="forward",
    )(pz, py, px, fld, obs)


def backward(pz, py, px, rat):
    return pl.pallas_call(
        backward_kernel,
        out_shape=jax.ShapeDtypeStruct((16, 64, 512), F32),
        in_specs=[SMEM] * 3 + [VM],
        out_specs=VM,
        scratch_shapes=TABLES + WORK,
        compiler_params=pltpu.CompilerParams(**PARAMS),
        name="backward",
    )(pz, py, px, rat)


def neighbours(shard):
    peers = lax.axis_size("slab")
    up = [(i, i + 1) for i in range(peers - 1)]
    down = [(j, i) for i, j in up]
    before = lax.ppermute(shard, "slab", up)
    after = lax.ppermute(shard, "slab", down)
    return jnp.concatenate([before, shard, after], axis=1)


def padded(taps):
    return jnp.pad(taps, ((0, 0), (0, 1)))


def local(estimate, observed, psf_z, psf_y, psf_x):
    pz, py, px = (padded(t[0]) for t in (psf_z, psf_y, psf_x))
    mine = jnp.swapaxes(estimate, 0, 1)
    copies = jnp.broadcast_to(mine, (lax.axis_size("view"), *mine.shape))
    field = lax.all_to_all(copies, "view", 0, 0, tiled=True).reshape(64, 16, 512)
    ratio = forward(pz, py, px, neighbours(field), observed[0])
    logs = backward(pz, py, px, neighbours(ratio))
    blocks = jnp.moveaxis(logs.reshape(16, 16, 4, 512), 1, 0)
    share = jnp.sum(lax.all_to_all(blocks, "view", 0, 0, tiled=True), axis=0)
    return estimate * jnp.exp(share)


def solution(mesh):
    placed = (
        P("slab", "view", None),
        P("view", "slab", None, None),
        P("view", None, None),
        P("view", None, None),
        P("view", None, None),
    )
    return jax.shard_map(
        local, mesh=mesh, in_specs=placed, out_specs=P("slab", "view", None), check_vma=False
    )
```

time: 397 us -> 266 us (0.67)
  the two profiles are of different devices: /device:TPU:25 before, /device:TPU:128 now
where the time goes in v1:
time: 266 us; the launch traced here: 265 us
  blocking collectives  123 us (46%)
  waiting for transfers between devices  61 us (23%)
  Pallas kernels  54.9 us (21%)
  starting transfers between devices  10.4 us (4%)
  other arithmetic  9.56 us (4%)
  local copies, waits for them, and re-layouts  5.96 us (2%)
    all_to_all x1, blocking collectives, local(): share = jnp.sum(lax.all_to_all(blocks, 'view', 0, 0, tiled=True), axis=0)  67.4 us
    all_to_all x1, blocking collectives, local(): lax.all_to_all(copies, 'view', 0, 0, tiled=True).reshape(64, 16, 512)  55.9 us
    ppermute x2, waiting for transfers between devices, neighbours(): after = lax.ppermute(shard, 'slab', down)  41.2 us
    pallas_call x1, Pallas kernels, forward(): pl.pallas_call(forward_kernel, out_shape=jax.ShapeDtypeStruct((64, 16, 51...  28.3 us
    pallas_call x1, Pallas kernels, backward(): pl.pallas_call(backward_kernel, out_shape=jax.ShapeDtypeStruct((16, 64, 5...  26.6 us
    ppermute x2, waiting for transfers between devices, neighbours(): before = lax.ppermute(shard, 'slab', up)  19.8 us
    concatenate x2, other arithmetic, neighbours(): return jnp.concatenate([before, shard, after], axis=1)  8.53 us
    ppermute x2, starting transfers between devices, neighbours(): after = lax.ppermute(shard, 'slab', down)  6.12 us
  transfers between devices with their start and end apart: 4, of which 4 were waited for; matrix products, arithmetic and copies ran while one was open for 1% of the time, Pallas kernels for 0%

profile of v1, /device:TPU:128, one launch (start us, length us, event | category | flops | bytes accessed | tf_op | source)
XLA Modules:
  0.0 265.3 jit_solution(11959492844810469174)
XLA Ops:
  0.0 0.9 copy.7
  1.0 0.2 broadcast_in_dim.3
  1.2 55.9 %all_to_all.10 = f32[16,4,16,512]{3,2,1,0:T(8,128)S(1)} all-to-all(f32[16,4,16,512]{3,2,1,0:T(8,128)S(1)} %broadcast_in_dim.3), channel_id=1, replica_groups=mesh['view'=16,'slab'=16] {'view'}, dimensions={0} | all-to-all | bytes 4194304 | tf_op jit(solution)/shard_map/all_to_all | solution.py:213
  57.2 4.2 %collective-permute-start.1 = (f32[64,16,512]{2,1,0:T(8,128)S(1)}, f32[64,16,512]{2,1,0:T(8,128)S(1)}, u32[]{:S(2)}, u32[]{:S(2)}) collective-permute-start(f32[64,16,512]{2,1,0:T(8,128)S(1)} %bitcast.19), channel_id=1, source_target_pairs={{1,0},{2,1},{3,2},{4,3},{5,4},{6,5},{7,6},{8,7},{9,8},{10,9},{11,1... | collective-permute-start | bytes 6291464 | tf_op jit(solution)/shard_map/ppermute | solution.py:201
  61.4 1.9 collective-permute-start
  63.3 0.6 pad.10.pz
  63.9 0.6 pad.11.py
  64.5 0.6 pad.12.px
  65.1 19.8 %collective-permute-done.1 = f32[64,16,512]{2,1,0:T(8,128)S(1)} collective-permute-done((f32[64,16,512]{2,1,0:T(8,128)S(1)}, f32[64,16,512]{2,1,0:T(8,128)S(1)}, u32[]{:S(2)}, u32[]{:S(2)}) %collective-permute-start.1) | collective-permute-done | bytes 2097184 | tf_op jit(solution)/shard_map/ppermute | solution.py:201
  84.9 9.9 %collective-permute-done = f32[64,16,512]{2,1,0:T(8,128)S(1)} collective-permute-done((f32[64,16,512]{2,1,0:T(8,128)S(1)}, f32[64,16,512]{2,1,0:T(8,128)S(1)}, u32[]{:S(2)}, u32[]{:S(2)}) %collective-permute-start) | collective-permute-done | bytes 2097184 | tf_op jit(solution)/shard_map/ppermute | solution.py:200
  94.8 3.4 %pad_maximum_fusion.fld = f32[64,48,512]{2,1,0:T(8,128)} fusion(f32[64,16,512]{2,1,0:T(8,128)S(1)} %collective-permute-done.1, f32[64,16,512]{2,1,0:T(8,128)S(1)} %bitcast.21, f32[64,16,512]{2,1,0:T(8,128)S(1)} %collective-permute-done), kind=kLoop, calls=%fused_computation | loop fusion | flops 3145728 | bytes 12582912 | tf_op jit(solution)/shard_map/concatenate | solution.py:202
  98.2 28.3 %forward.1 = f32[64,16,512]{2,1,0:T(8,128)} custom-call(f32[3,32]{1,0:T(4,128)} %pad.10.pz, f32[3,32]{1,0:T(4,128)} %pad.11.py, f32[3,32]{1,0:T(4,128)} %pad.12.px, f32[64,48,512]{2,1,0:T(8,128)} %pad_maximum_fusion.fld, f32[16,64,512]{2,1,0:T(8,128)} %bitcast.22), custom_call_target="tpu_custom_call" | custom-call | tf_op jit(solution)/shard_map/forward/pallas_call | solution.py:173
  126.5 1.9 collective-permute-start.3
  128.5 2.4 collective-permute-start.2
  130.9 21.4 %collective-permute-done.3 = f32[64,16,512]{2,1,0:T(8,128)S(1)} collective-permute-done((f32[64,16,512]{2,1,0:T(8,128)}, f32[64,16,512]{2,1,0:T(8,128)S(1)}, u32[]{:S(2)}, u32[]{:S(2)}) %collective-permute-start.3) | collective-permute-done | bytes 2097184 | tf_op jit(solution)/shard_map/ppermute | solution.py:201
  152.3 9.8 %collective-permute-done.2 = f32[64,16,512]{2,1,0:T(8,128)S(1)} collective-permute-done((f32[64,16,512]{2,1,0:T(8,128)}, f32[64,16,512]{2,1,0:T(8,128)S(1)}, u32[]{:S(2)}, u32[]{:S(2)}) %collective-permute-start.2) | collective-permute-done | bytes 2097184 | tf_op jit(solution)/shard_map/ppermute | solution.py:200
  162.1 5.2 %pad_maximum_fusion.1.rat = f32[64,48,512]{2,1,0:T(8,128)} fusion(f32[64,16,512]{2,1,0:T(8,128)S(1)} %collective-permute-done.3, f32[64,16,512]{2,1,0:T(8,128)} %forward.1, f32[64,16,512]{2,1,0:T(8,128)S(1)} %collective-permute-done.2), kind=kLoop, calls=%fused_computation.1 | loop fusion | flops 3145728 | bytes 12582912 | tf_op jit(solution)/shard_map/concatenate | solution.py:202
  167.3 26.6 %backward.1 = f32[16,64,512]{2,1,0:T(8,128)} custom-call(f32[3,32]{1,0:T(4,128)} %pad.10.pz, f32[3,32]{1,0:T(4,128)} %pad.11.py, f32[3,32]{1,0:T(4,128)} %pad.12.px, f32[64,48,512]{2,1,0:T(8,128)} %pad_maximum_fusion.1.rat), custom_call_target="tpu_custom_call" | custom-call | tf_op jit(solution)/shard_map/backward/pallas_call | solution.py:185
  193.9 1.9 reshape.7
  195.8 0.5 copy.16
  196.3 67.4 %all_to_all.11 = f32[16,16,4,512]{3,2,1,0:T(4,128)S(1)} all-to-all(f32[16,16,4,512]{3,2,1,0:T(4,128)S(1)} %bitcast.18), channel_id=1, replica_groups=mesh['view'=16,'slab'=16] {'view'}, dimensions={0} | all-to-all | bytes 4194304 | tf_op jit(solution)/shard_map/all_to_all | solution.py:217
  263.7 0.3 reduce_sum.9
  264.0 0.6 copy-done
  264.6 0.7 exponential_multiply_fusion
  (10 shorter events, 0.0 us)
Async XLA Ops:
  1.2 62.1 %copy-start.1 = (f32[1,3,31]{2,0,1:T(1,128)S(1)}, f32[1,3,31]{2,0,1:T(1,128)}, u32[]{:S(2)}) copy-start(f32[1,3,31]{2,0,1:T(1,128)} %param.7) | copy-start | bytes 1120
  1.2 62.1 %copy-start.2 = (f32[1,3,31]{2,0,1:T(1,128)S(1)}, f32[1,3,31]{2,0,1:T(1,128)}, u32[]{:S(2)}) copy-start(f32[1,3,31]{2,0,1:T(1,128)} %param.8) | copy-start | bytes 1120
  1.2 63.3 %copy-start.3 = (f32[1,3,31]{2,0,1:T(1,128)S(1)}, f32[1,3,31]{2,0,1:T(1,128)}, u32[]{:S(2)}) copy-start(f32[1,3,31]{2,0,1:T(1,128)} %param.9) | copy-start | bytes 1120
  57.2 27.8 %collective-permute-start.1 = (f32[64,16,512]{2,1,0:T(8,128)S(1)}, f32[64,16,512]{2,1,0:T(8,128)S(1)}, u32[]{:S(2)}, u32[]{:S(2)}) collective-permute-start(f32[64,16,512]{2,1,0:T(8,128)S(1)} %bitcast.19), channel_id=1, source_target_pairs={{1,0},{2,1},{3,2},{4,3},{5,4},{6,5},{7,6},{8,7},{9,8},{10,9},{11,1... | collective-permute-start | bytes 6291464 | tf_op jit(solution)/shard_map/ppermute | solution.py:201
  61.4 33.5 %collective-permute-start = (f32[64,16,512]{2,1,0:T(8,128)S(1)}, f32[64,16,512]{2,1,0:T(8,128)S(1)}, u32[]{:S(2)}, u32[]{:S(2)}) collective-permute-start(f32[64,16,512]{2,1,0:T(8,128)S(1)} %bitcast.20), channel_id=1, source_target_pairs={{0,1},{1,2},{2,3},{3,4},{4,5},{5,6},{6,7},{7,8},{8,9},{9,10},{10,1... | collective-permute-start | bytes 6291464 | tf_op jit(solution)/shard_map/ppermute | solution.py:200
  126.5 25.8 %collective-permute-start.3 = (f32[64,16,512]{2,1,0:T(8,128)}, f32[64,16,512]{2,1,0:T(8,128)S(1)}, u32[]{:S(2)}, u32[]{:S(2)}) collective-permute-start(f32[64,16,512]{2,1,0:T(8,128)} %forward.1), channel_id=1, source_target_pairs={{1,0},{2,1},{3,2},{4,3},{5,4},{6,5},{7,6},{8,7},{9,8},{10,9},{11,1... | collective-permute-start | bytes 6291464 | tf_op jit(solution)/shard_map/ppermute | solution.py:201
  128.5 33.7 %collective-permute-start.2 = (f32[64,16,512]{2,1,0:T(8,128)}, f32[64,16,512]{2,1,0:T(8,128)S(1)}, u32[]{:S(2)}, u32[]{:S(2)}) collective-permute-start(f32[64,16,512]{2,1,0:T(8,128)} %forward.1), channel_id=1, source_target_pairs={{0,1},{1,2},{2,3},{3,4},{4,5},{5,6},{6,7},{7,8},{8,9},{9,10},{10,1... | collective-permute-start | bytes 6291464 | tf_op jit(solution)/shard_map/ppermute | solution.py:200
  263.7 0.9 copy-start

commit v2 on v1

--- a/solution.py
+++ b/solution.py
@@ -70,7 +70,7 @@
 
 def z_stage(src, wz, thi, tlo, unroll=4):
     def one(y, _):
-        hi, lo = split(src[y])
+        hi, lo = split(jnp.concatenate([src[b, y] for b in range(4)], axis=1))
         o = dot(wz[...], jnp.concatenate([hi, lo], axis=0))
         hi, lo = split(o[:48] + o[48:])
         thi[y] = hi
@@ -125,81 +125,316 @@
     lax.fori_loop(lo, hi, one, 0)
 
 
+SLABS, GROUP = 16, 4
+MESH = pl.DeviceIdType.MESH
+
+
+def remote(src, dst, send, recv, device):
+    return pltpu.make_async_remote_copy(
+        src_ref=src, dst_ref=dst, send_sem=send, recv_sem=recv, device_id=device, device_id_type=MESH
+    )
+
+
+def z_rows(src, wz, thi, tlo, start, count):
+    for i in range(count):
+        y = start + i
+        hi, lo = split(src[y])
+        o = dot(wz[...], jnp.concatenate([hi, lo], axis=0))
+        hi, lo = split(o[:48] + o[48:])
+        thi[y] = hi
+        tlo[y] = lo
+
+
+def kernel(
+    pz, py, px, est, obs_hbm, out,
+    fld, rat, obs, thi, tlo, xo, logs, xin, zout, zin,
+    wzf, wyf, cxf, exf, wzb, wyb, cxb, exb,
+    obs_sem, main_recv, lo_recv, hi_recv, cross_recv,
+    zsend, xsend, upsend, dnsend, csend, czsend, cxsend,
+    rup_send, rdn_send, rlo_recv, rhi_recv,
+    sx_send, sx_recv, sz_send, sz_recv,
+):
+    v, s = lax.axis_index("view"), lax.axis_index("slab")
+    x, zl = lax.div(v, GROUP), lax.rem(v, GROUP)
+    zpeer = [x * GROUP + lax.rem(zl + i, GROUP) for i in range(1, GROUP)]
+    xs = [lax.rem(x + i, GROUP) for i in (1, 3, 2)]
+    xpeer = [a * GROUP + zl for a in xs]
+    lower, upper = s > 0, s < SLABS - 1
+    cross_lo, cross_hi = s == SLABS // 2, s == SLABS // 2 - 1
+    cross = jnp.logical_or(cross_lo, cross_hi)
+    near_lo = jnp.logical_and(lower, jnp.logical_not(cross_lo))
+    near_hi = jnp.logical_and(upper, jnp.logical_not(cross_hi))
+    my_off = pl.multiple_of(jnp.where(cross_lo, 0, 32), 16)
+    far_off = pl.multiple_of(jnp.where(cross_lo, 32, 0), 16)
+    far_slab = jnp.where(cross_lo, s - 1, s + 1)
+
+    def block(shard, off):
+        return fld.at[pl.ds(shard * 4, 4), pl.ds(off, 16), :]
+
+    for q in range(4):
+        fld[v * 4 + q, 16:32, :] = est[:, q, :]
+
+    barrier = pltpu.get_barrier_semaphore()
+    for peer in zpeer + xpeer:
+        pl.semaphore_signal(barrier, inc=1, device_id=(peer, s), device_id_type=MESH)
+
+    @pl.when(lower)
+    def _():
+        pl.semaphore_signal(barrier, inc=1, device_id=(v, s - 1), device_id_type=MESH)
+
+    @pl.when(upper)
+    def _():
+        pl.semaphore_signal(barrier, inc=1, device_id=(v, s + 1), device_id_type=MESH)
+
+    pl.semaphore_wait(barrier, 6 + jnp.where(lower, 1, 0) + jnp.where(upper, 1, 0))
+
+    def to_z(shard, off, i, sends, recv):
+        return remote(block(shard, off), block(shard, off), sends.at[i], recv.at[shard], (zpeer[i], s))
+
+    def to_x(shard, off, k, i, sends, recv):
+        return remote(block(shard, off), block(shard, off), sends.at[k, i], recv.at[shard], (xpeer[i], s))
+
+    def to_up(shard, k):
+        return remote(block(shard, 16), block(shard, 0), upsend.at[k], lo_recv.at[shard], (v, s + 1))
+
+    def to_dn(shard, k):
+        return remote(block(shard, 16), block(shard, 32), dnsend.at[k], hi_recv.at[shard], (v, s - 1))
+
+    def to_far():
+        return remote(block(v, 16), block(v, far_off), csend.at[0], cross_recv.at[v], (v, far_slab))
+
+    def halo(shard, k):
+        @pl.when(near_hi)
+        def _():
+            to_up(shard, k).start()
+
+        @pl.when(near_lo)
+        def _():
+            to_dn(shard, k).start()
+
+    near = [v] + zpeer
+    groups = [near] + [[xs[j] * GROUP + lax.rem(zl + i, GROUP) for i in range(GROUP)] for j in range(3)]
+
+    @pl.when(cross)
+    def _():
+        to_far().start()
+
+    for i in range(3):
+        to_z(v, 16, i, zsend, main_recv).start()
+    for i in range(3):
+        to_x(v, 16, 0, i, xsend, main_recv).start()
+    halo(v, 0)
+    load = pltpu.make_async_copy(obs_hbm, obs, obs_sem.at[0])
+    load.start()
+
+    @pl.when(s == 0)
+    def _():
+        fld[:, 0:16, :] = jnp.zeros((64, 16, 512), F32)
+        rat[:, :, 0:16, :] = jnp.zeros((4, 64, 16, 128), F32)
+
+    @pl.when(s == SLABS - 1)
+    def _():
+        fld[:, 32:48, :] = jnp.zeros((64, 16, 512), F32)
+        rat[:, :, 32:48, :] = jnp.zeros((4, 64, 16, 128), F32)
+
+    build_tables(pz, py, px, wzf, wyf, cxf, exf, False)
+
+    for k in range(1, 4):
+        shard = near[k]
+        to_z(shard, 16, 0, zsend, main_recv).wait_recv()
+        for i in range(3):
+            to_x(shard, 16, k, i, xsend, main_recv).start()
+        halo(shard, k)
+
+    @pl.when(cross)
+    def _():
+        to_far().wait_recv()
+        for i in range(3):
+            to_z(v, my_off, i, czsend, cross_recv).start()
+        for i in range(3):
+            to_x(v, my_off, 0, i, cxsend, cross_recv).start()
+
+    def take(g):
+        for k in range(4):
+            shard = groups[g][k]
+            to_x(shard, 16, k, 0, xsend, main_recv).wait_recv()
+            halo(shard, 4 * g + k)
+
+    def z_group(g):
+        def one(k, _):
+            shard = groups[g][0] - zl + lax.rem(zl + k, GROUP)
+
+            @pl.when(near_lo)
+            def _():
+                to_up(shard, 0).wait_recv()
+
+            @pl.when(near_hi)
+            def _():
+                to_dn(shard, 0).wait_recv()
+
+            if g > 0:
+
+                @pl.when(cross)
+                def _():
+                    to_x(shard, my_off, 0, 0, cxsend, cross_recv).wait_recv()
+
+            z_rows(fld, wzf, thi, tlo, shard * 4, 4)
+            return 0
+
+        lax.fori_loop(0, GROUP, one, 0)
+
+    take(1)
+
+    @pl.when(cross)
+    def _():
+        for k in range(1, 4):
+            shard = near[k]
+            to_z(shard, my_off, 0, czsend, cross_recv).wait_recv()
+            for i in range(3):
+                to_x(shard, my_off, k, i, cxsend, cross_recv).start()
+
+    z_group(0)
+    take(2)
+    z_group(1)
+    take(3)
+    z_group(2)
+    z_group(3)
+
+    x_stage(thi, tlo, cxf, exf, xo)
+    load.wait()
+
+    def to_ratio(z, blurred):
+        ratio = obs[z] / blurred
+        for b in range(4):
+            rows = rat.at[b].reshape(3072, 128)
+            rows[pl.ds(z + 16, 64, stride=48), :] = ratio[:, 128 * b : 128 * b + 128]
+
+    def up_ratio(c):
+        src, dst = (rat.at[:, :, pl.ds(o + 8 * c, 8), :] for o in (16, 0))
+        return remote(src, dst, rup_send.at[c], rlo_recv.at[c], (v, s + 1))
+
+    def dn_ratio(c):
+        src, dst = (rat.at[:, :, pl.ds(o + 8 * c, 8), :] for o in (16, 32))
+        return remote(src, dst, rdn_send.at[c], rhi_recv.at[c], (v, s - 1))
+
+    for c in range(2):
+        y_stage(xo, wyf, to_ratio, 8 * c, 8 * c + 8)
+
+        @pl.when(upper)
+        def _():
+            up_ratio(c).start()
+
+        @pl.when(lower)
+        def _():
+            dn_ratio(c).start()
+
+    build_tables(pz, py, px, wzb, wyb, cxb, exb, True)
+
+    for c in range(2):
+
+        @pl.when(lower)
+        def _():
+            up_ratio(c).wait_recv()
+
+        @pl.when(upper)
+        def _():
+            dn_ratio(c).wait_recv()
+
+    z_stage(rat, wzb, thi, tlo)
+    x_stage(thi, tlo, cxb, exb, xo)
+
+    def to_log(z, back):
+        logs[z] = jnp.log(back)
+
+    def share_x(c, i):
+        src = logs.at[pl.ds(4 * c, 4), pl.ds(pl.multiple_of(xs[i] * 16, 16), 16), :]
+        return remote(src, xin.at[i, pl.ds(4 * c, 4)], sx_send.at[c, i], sx_recv.at[c, i], (xpeer[i], s))
+
+    def share_z(c, i):
+        j = lax.rem(zl + i + 1, GROUP)
+        src = zout.at[j, pl.ds(16 * c, 16), :]
+        return remote(src, zin.at[i, pl.ds(16 * c, 16), :], sz_send.at[c, i], sz_recv.at[c, i], (zpeer[i], s))
+
+    def reduce_x(c):
+        for i in range(3):
+            share_x(c, i).wait_recv()
+        for q in range(4):
+            z = 4 * c + q
+            total = logs[z, pl.ds(pl.multiple_of(x * 16, 16), 16), :]
+            for i in range(3):
+                total = total + xin[i, z]
+            for j in range(4):
+                zout[j, 4 * z : 4 * z + 4, :] = total[4 * j : 4 * j + 4]
+        for i in range(3):
+            share_z(c, i).start()
+
+    def final(c):
+        for i in range(3):
+            share_z(c, i).wait_recv()
+        for q in range(4):
+            z = 4 * c + q
+            rows = pl.ds(4 * z, 4)
+            total = zout[zl, rows, :]
+            for i in range(3):
+                total = total + zin[i, rows, :]
+            out[z] = est[z] * jnp.exp(total)
+
+    for c in range(4):
+        y_stage(xo, wyb, to_log, 4 * c, 4 * c + 4)
+        for i in range(3):
+            share_x(c, i).start()
+    for c in range(4):
+        reduce_x(c)
+    for c in range(4):
+        final(c)
+
+    for i in range(3):
+        to_z(v, 16, i, zsend, main_recv).wait_send()
+        for k in range(4):
+            to_x(v, 16, k, i, xsend, main_recv).wait_send()
+        for c in range(4):
+            share_x(c, i).wait_send()
+            share_z(c, i).wait_send()
+
+    @pl.when(cross)
+    def _():
+        to_far().wait_send()
+        for i in range(3):
+            to_z(v, my_off, i, czsend, cross_recv).wait_send()
+            for k in range(4):
+                to_x(v, my_off, k, i, cxsend, cross_recv).wait_send()
+
+    @pl.when(near_hi)
+    def _():
+        for k in range(16):
+            to_up(v, k).wait_send()
+
+    @pl.when(near_lo)
+    def _():
+        for k in range(16):
+            to_dn(v, k).wait_send()
+
+    @pl.when(upper)
+    def _():
+        for c in range(2):
+            up_ratio(c).wait_send()
+
+    @pl.when(lower)
+    def _():
+        for c in range(2):
+            dn_ratio(c).wait_send()
+
+
 TABLES = [
     pltpu.VMEM((96, 96), BF16),
     pltpu.VMEM((128, 384), BF16),
     pltpu.VMEM((3, 256, 256), BF16),
     pltpu.VMEM((3, 256, 256), BF16),
 ]
-WORK = [
-    pltpu.VMEM((64, 48, 512), BF16),
-    pltpu.VMEM((64, 48, 512), BF16),
-    pltpu.VMEM((4, 3072, 128), F32),
-]
-
-
-def forward_kernel(pz, py, px, fld, obs, out, wz, wy, cx, ex, thi, tlo, xo, rat):
-    build_tables(pz, py, px, wz, wy, cx, ex, False)
-    z_stage(fld, wz, thi, tlo)
-    x_stage(thi, tlo, cx, ex, xo)
-
-    def finish(z, blurred):
-        ratio = obs[z] / blurred
-        for b in range(4):
-            rat[b, pl.ds(z, 64, stride=16), :] = ratio[:, 128 * b : 128 * b + 128]
-
-    y_stage(xo, wy, finish)
-    for b in range(4):
-        out[:, :, 128 * b : 128 * b + 128] = rat[b].reshape(64, 16, 128)
-
-
-def backward_kernel(pz, py, px, rat, out, wz, wy, cx, ex, thi, tlo, xo):
-    build_tables(pz, py, px, wz, wy, cx, ex, True)
-    z_stage(rat, wz, thi, tlo)
-    x_stage(thi, tlo, cx, ex, xo)
-
-    def finish(z, back):
-        out[z] = jnp.log(back)
-
-    y_stage(xo, wy, finish)
-
-
+DMA = pltpu.SemaphoreType.DMA
 SMEM = pl.BlockSpec(memory_space=pltpu.SMEM)
 VM = pl.BlockSpec(memory_space=pltpu.VMEM)
-PARAMS = dict(vmem_limit_bytes=60 << 20)
-
-
-def forward(pz, py, px, fld, obs):
-    return pl.pallas_call(
-        forward_kernel,
-        out_shape=jax.ShapeDtypeStruct((64, 16, 512), F32),
-        in_specs=[SMEM] * 3 + [VM] * 2,
-        out_specs=VM,
-        scratch_shapes=TABLES + WORK + [pltpu.VMEM((4, 1024, 128), F32)],
-        compiler_params=pltpu.CompilerParams(**PARAMS),
-        name="forward",
-    )(pz, py, px, fld, obs)
-
-
-def backward(pz, py, px, rat):
-    return pl.pallas_call(
-        backward_kernel,
-        out_shape=jax.ShapeDtypeStruct((16, 64, 512), F32),
-        in_specs=[SMEM] * 3 + [VM],
-        out_specs=VM,
-        scratch_shapes=TABLES + WORK,
-        compiler_params=pltpu.CompilerParams(**PARAMS),
-        name="backward",
-    )(pz, py, px, rat)
-
-
-def neighbours(shard):
-    peers = lax.axis_size("slab")
-    up = [(i, i + 1) for i in range(peers - 1)]
-    down = [(j, i) for i, j in up]
-    before = lax.ppermute(shard, "slab", up)
-    after = lax.ppermute(shard, "slab", down)
-    return jnp.concatenate([before, shard, after], axis=1)
+ANY = pl.BlockSpec(memory_space=pl.ANY)
 
 
 def padded(taps):
@@ -208,14 +443,34 @@
 
 def local(estimate, observed, psf_z, psf_y, psf_x):
     pz, py, px = (padded(t[0]) for t in (psf_z, psf_y, psf_x))
-    mine = jnp.swapaxes(estimate, 0, 1)
-    copies = jnp.broadcast_to(mine, (lax.axis_size("view"), *mine.shape))
-    field = lax.all_to_all(copies, "view", 0, 0, tiled=True).reshape(64, 16, 512)
-    ratio = forward(pz, py, px, neighbours(field), observed[0])
-    logs = backward(pz, py, px, neighbours(ratio))
-    blocks = jnp.moveaxis(logs.reshape(16, 16, 4, 512), 1, 0)
-    share = jnp.sum(lax.all_to_all(blocks, "view", 0, 0, tiled=True), axis=0)
-    return estimate * jnp.exp(share)
+    return pl.pallas_call(
+        kernel,
+        out_shape=jax.ShapeDtypeStruct(estimate.shape, F32),
+        in_specs=[SMEM] * 3 + [VM, ANY],
+        out_specs=VM,
+        scratch_shapes=[
+            pltpu.VMEM((64, 48, 512), F32),
+            pltpu.VMEM((4, 64, 48, 128), F32),
+            pltpu.VMEM((16, 64, 512), F32),
+            pltpu.VMEM((64, 48, 512), BF16),
+            pltpu.VMEM((64, 48, 512), BF16),
+            pltpu.VMEM((4, 3072, 128), F32),
+            pltpu.VMEM((16, 64, 512), F32),
+            pltpu.VMEM((3, 16, 16, 512), F32),
+            pltpu.VMEM((4, 64, 512), F32),
+            pltpu.VMEM((3, 64, 512), F32),
+        ]
+        + TABLES * 2
+        + [DMA((1,))]
+        + [DMA((16,))] * 4
+        + [DMA((3,)), DMA((4, 3)), DMA((16,)), DMA((16,)), DMA((1,)), DMA((3,)), DMA((4, 3))]
+        + [DMA((2,))] * 4
+        + [DMA((4, 3))] * 4,
+        compiler_params=pltpu.CompilerParams(
+            collective_id=0, has_side_effects=True, vmem_limit_bytes=60 << 20
+        ),
+        name="deconvolve",
+    )(pz, py, px, estimate, observed[0])
 
 
 def solution(mesh):

time: 266 us -> 150 us (0.56)
  the two profiles are of different devices: /device:TPU:128 before, /device:TPU:25 now
where the time goes in v2:
time: 150 us
  Pallas kernels  145 us (97%)
  local copies, waits for them, and re-layouts  5.39 us (4%)
    pallas_call x1, Pallas kernels, local(): pl.pallas_call(kernel, out_shape=jax.ShapeDtypeStruct(estimate.shape, F32...  145 us
    unnamed x4, local copies, waits for them, and re-layouts  3.61 us

profile of v2, /device:TPU:25, one launch (start us, length us, event | category | flops | bytes accessed | tf_op | source)
XLA Modules:
  0.0 150.2 jit_solution(5931642639923006370)
XLA Ops:
  0.0 0.7 copy.14
  0.7 0.6 pad.10.pz
  1.3 0.7 copy.13
  1.9 0.6 pad.11.py
  2.5 0.7 copy.12
  3.2 0.6 pad.12.px
  3.8 144.8 %deconvolve.1 = f32[16,4,512]{2,1,0:T(4,128)} custom-call(f32[3,32]{1,0:T(4,128)} %pad.10.pz, f32[3,32]{1,0:T(4,128)} %pad.11.py, f32[3,32]{1,0:T(4,128)} %pad.12.px, f32[16,4,512]{2,1,0:T(4,128)} %est.1, f32[16,64,512]{2,1,0:T(8,128)} %bitcast.10), custom_call_target="tpu_custom_call" | custom-call | tf_op jit(solution)/shard_map/deconvolve/pallas_call | solution.py:446
  148.6 1.6 %copy.16 = f32[16,4,512]{2,1,0:T(4,128)} copy(f32[16,4,512]{2,1,0:T(4,128)} %deconvolve.1) | data formatting | bytes 262144

commit v3 on v2

--- a/solution.py
+++ b/solution.py
@@ -147,18 +147,21 @@
 
 def kernel(
     pz, py, px, est, obs_hbm, out,
-    fld, rat, obs, thi, tlo, xo, logs, xin, zout, zin,
+    fld, rat, relay, obs, thi, tlo, xo, logs, xin, zout, zin,
     wzf, wyf, cxf, exf, wzb, wyb, cxb, exb,
-    obs_sem, main_recv, lo_recv, hi_recv, cross_recv,
-    zsend, xsend, upsend, dnsend, csend, czsend, cxsend,
+    obs_sem, lo_recv, hi_recv, upsend, dnsend, far_send, far_recv,
+    mz_send, mz_recv, mx_send, mx_recv, mc_send, mc_recv,
+    cz_send, cz_recv, cx_send, cx_recv, cc_send, cc_recv,
     rup_send, rdn_send, rlo_recv, rhi_recv,
+    rel_send, rel_recv, fwd_send, fwd_recv,
     sx_send, sx_recv, sz_send, sz_recv,
 ):
     v, s = lax.axis_index("view"), lax.axis_index("slab")
     x, zl = lax.div(v, GROUP), lax.rem(v, GROUP)
-    zpeer = [x * GROUP + lax.rem(zl + i, GROUP) for i in range(1, GROUP)]
-    xs = [lax.rem(x + i, GROUP) for i in (1, 3, 2)]
-    xpeer = [a * GROUP + zl for a in xs]
+    zs = [zl, zl + 1 - 2 * lax.rem(zl, 2), lax.rem(zl + 2, GROUP), 3 - zl]
+    xs = [x, x + 1 - 2 * lax.rem(x, 2), 3 - x, lax.rem(x + 2, GROUP)]
+    zpeer = [x * GROUP + a for a in zs[1:]]
+    xpeer = [a * GROUP + zl for a in xs[1:]]
     lower, upper = s > 0, s < SLABS - 1
     cross_lo, cross_hi = s == SLABS // 2, s == SLABS // 2 - 1
     cross = jnp.logical_or(cross_lo, cross_hi)
@@ -167,6 +170,10 @@
     my_off = pl.multiple_of(jnp.where(cross_lo, 0, 32), 16)
     far_off = pl.multiple_of(jnp.where(cross_lo, 32, 0), 16)
     far_slab = jnp.where(cross_lo, s - 1, s + 1)
+    bottom, top = s == 0, s == SLABS - 1
+    relays = jnp.logical_or(bottom, top)
+    relay_to = jnp.where(bottom, SLABS // 2, SLABS // 2 - 1)
+    my_relay = jnp.where(cross_lo, SLABS - 1, 0)
 
     def block(shard, off):
         return fld.at[pl.ds(shard * 4, 4), pl.ds(off, 16), :]
@@ -186,44 +193,85 @@
     def _():
         pl.semaphore_signal(barrier, inc=1, device_id=(v, s + 1), device_id_type=MESH)
 
-    pl.semaphore_wait(barrier, 6 + jnp.where(lower, 1, 0) + jnp.where(upper, 1, 0))
-
-    def to_z(shard, off, i, sends, recv):
-        return remote(block(shard, off), block(shard, off), sends.at[i], recv.at[shard], (zpeer[i], s))
-
-    def to_x(shard, off, k, i, sends, recv):
-        return remote(block(shard, off), block(shard, off), sends.at[k, i], recv.at[shard], (xpeer[i], s))
-
-    def to_up(shard, k):
-        return remote(block(shard, 16), block(shard, 0), upsend.at[k], lo_recv.at[shard], (v, s + 1))
-
-    def to_dn(shard, k):
-        return remote(block(shard, 16), block(shard, 32), dnsend.at[k], hi_recv.at[shard], (v, s - 1))
+    @pl.when(relays)
+    def _():
+        for peer in (SLABS // 2 - 1, SLABS // 2):
+            pl.semaphore_signal(barrier, inc=1, device_id=(v, peer), device_id_type=MESH)
+
+    @pl.when(cross)
+    def _():
+        for peer in (0, SLABS - 1):
+            pl.semaphore_signal(barrier, inc=1, device_id=(v, peer), device_id_type=MESH)
+
+    extra = jnp.where(jnp.logical_or(relays, cross), 2, 0)
+    pl.semaphore_wait(barrier, extra + 6 + jnp.where(lower, 1, 0) + jnp.where(upper, 1, 0))
+
+    def shard(j, k):
+        return xs[j] * GROUP + zs[k]
+
+    def half(which, off, h):
+        return fld.at[pl.ds(which * 4 + 2 * h, 2), pl.ds(off, 16), :]
+
+    main = (16, mz_send, mz_recv, mx_send, mx_recv, mc_send, mc_recv)
+    side = (my_off, cz_send, cz_recv, cx_send, cx_recv, cc_send, cc_recv)
+
+    def to_z(stream, i):
+        ref = block(v, stream[0])
+        return remote(ref, ref, stream[1].at[i], stream[2].at[i], (zpeer[i], s))
+
+    def to_x(stream, i, k, which):
+        ref = block(which, stream[0])
+        return remote(ref, ref, stream[3].at[i, k], stream[4].at[i, k], (xpeer[i], s))
+
+    def on_x(stream, h, k, which):
+        ref = half(which, stream[0], h)
+        return remote(ref, ref, stream[5].at[h, k], stream[6].at[h, k], (xpeer[1 - h], s))
+
+    def to_up(which, n):
+        return remote(block(which, 16), block(which, 0), upsend.at[n], lo_recv.at[n], (v, s + 1))
+
+    def to_dn(which, n):
+        return remote(block(which, 16), block(which, 32), dnsend.at[n], hi_recv.at[n], (v, s - 1))
 
     def to_far():
-        return remote(block(v, 16), block(v, far_off), csend.at[0], cross_recv.at[v], (v, far_slab))
-
-    def halo(shard, k):
-        @pl.when(near_hi)
-        def _():
-            to_up(shard, k).start()
-
-        @pl.when(near_lo)
-        def _():
-            to_dn(shard, k).start()
-
-    near = [v] + zpeer
-    groups = [near] + [[xs[j] * GROUP + lax.rem(zl + i, GROUP) for i in range(GROUP)] for j in range(3)]
+        return remote(block(v, 16), block(v, far_off), far_send.at[0], far_recv.at[0], (v, far_slab))
+
+    def halo(stream, j, k):
+        if stream is main:
+
+            @pl.when(near_hi)
+            def _():
+                to_up(shard(j, k), 4 * j + k).start()
+
+            @pl.when(near_lo)
+            def _():
+                to_dn(shard(j, k), 4 * j + k).start()
+
+    def take_near(stream, k):
+        if k > 0:
+            to_z(stream, k - 1).wait_recv()
+        for i in range(2):
+            to_x(stream, i, k, shard(0, k)).start()
+        halo(stream, 0, k)
+
+    def take_x(stream, k):
+        for i in range(2):
+            to_x(stream, i, k, shard(1 + i, k)).wait_recv()
+            on_x(stream, i, k, shard(1 + i, k)).start()
+            halo(stream, 1 + i, k)
+
+    def take_far(stream, k):
+        for h in range(2):
+            on_x(stream, h, k, shard(3, k)).wait_recv()
+        halo(stream, 3, k)
 
     @pl.when(cross)
     def _():
         to_far().start()
 
     for i in range(3):
-        to_z(v, 16, i, zsend, main_recv).start()
-    for i in range(3):
-        to_x(v, 16, 0, i, xsend, main_recv).start()
-    halo(v, 0)
+        to_z(main, i).start()
+    take_near(main, 0)
     load = pltpu.make_async_copy(obs_hbm, obs, obs_sem.at[0])
     load.start()
 
@@ -239,64 +287,55 @@
 
     build_tables(pz, py, px, wzf, wyf, cxf, exf, False)
 
-    for k in range(1, 4):
-        shard = near[k]
-        to_z(shard, 16, 0, zsend, main_recv).wait_recv()
-        for i in range(3):
-            to_x(shard, 16, k, i, xsend, main_recv).start()
-        halo(shard, k)
+    def z_group(k):
+        for j in range(4):
+
+            @pl.when(near_lo)
+            def _():
+                to_up(v, 4 * j + k).wait_recv()
+
+            @pl.when(near_hi)
+            def _():
+                to_dn(v, 4 * j + k).wait_recv()
+
+        def one(j, _):
+            first = lax.rem(xs[0] + j, GROUP) * GROUP + zs[k]
+            z_rows(fld, wzf, thi, tlo, first * 4, 4)
+            return 0
+
+        lax.fori_loop(0, GROUP, one, 0)
+
+    def crossing(*steps):
+        @pl.when(cross)
+        def _():
+            for step, k in steps:
+                step(side, k)
+
+    take_near(main, 1)
+    take_x(main, 0)
+    take_near(main, 2)
+    take_near(main, 3)
 
     @pl.when(cross)
     def _():
         to_far().wait_recv()
         for i in range(3):
-            to_z(v, my_off, i, czsend, cross_recv).start()
-        for i in range(3):
-            to_x(v, my_off, 0, i, cxsend, cross_recv).start()
-
-    def take(g):
-        for k in range(4):
-            shard = groups[g][k]
-            to_x(shard, 16, k, 0, xsend, main_recv).wait_recv()
-            halo(shard, 4 * g + k)
-
-    def z_group(g):
-        def one(k, _):
-            shard = groups[g][0] - zl + lax.rem(zl + k, GROUP)
-
-            @pl.when(near_lo)
-            def _():
-                to_up(shard, 0).wait_recv()
-
-            @pl.when(near_hi)
-            def _():
-                to_dn(shard, 0).wait_recv()
-
-            if g > 0:
-
-                @pl.when(cross)
-                def _():
-                    to_x(shard, my_off, 0, 0, cxsend, cross_recv).wait_recv()
-
-            z_rows(fld, wzf, thi, tlo, shard * 4, 4)
-            return 0
-
-        lax.fori_loop(0, GROUP, one, 0)
-
-    take(1)
-
-    @pl.when(cross)
-    def _():
-        for k in range(1, 4):
-            shard = near[k]
-            to_z(shard, my_off, 0, czsend, cross_recv).wait_recv()
-            for i in range(3):
-                to_x(shard, my_off, k, i, cxsend, cross_recv).start()
-
+            to_z(side, i).start()
+        take_near(side, 0)
+
+    take_far(main, 0)
+    take_x(main, 1)
+    crossing((take_near, 1), (take_x, 0))
+    take_far(main, 1)
+    take_x(main, 2)
+    crossing((take_near, 2), (take_near, 3), (take_far, 0), (take_x, 1))
     z_group(0)
-    take(2)
+    take_far(main, 2)
+    take_x(main, 3)
+    crossing((take_x, 2), (take_far, 1))
     z_group(1)
-    take(3)
+    take_far(main, 3)
+    crossing((take_x, 3), (take_far, 2), (take_far, 3))
     z_group(2)
     z_group(3)
 
@@ -317,14 +356,33 @@
         src, dst = (rat.at[:, :, pl.ds(o + 8 * c, 8), :] for o in (16, 32))
         return remote(src, dst, rdn_send.at[c], rhi_recv.at[c], (v, s - 1))
 
+    def rows_of(off, c, h):
+        return rat.at[:, pl.ds(32 * h, 32), pl.ds(pl.multiple_of(off + 8 * c, 8), 8), :]
+
+    def far_ratio(c):
+        src, dst = rows_of(16, c, 0), rows_of(far_off, c, 0)
+        return remote(src, dst, far_send.at[1 + c], far_recv.at[1 + c], (v, far_slab))
+
+    def to_relay(c):
+        return remote(rows_of(16, c, 1), relay.at[c], rel_send.at[c], rel_recv.at[c], (v, my_relay))
+
+    def from_relay(c):
+        dst = rows_of(jnp.where(bottom, 0, 32), c, 1)
+        return remote(relay.at[c], dst, fwd_send.at[c], fwd_recv.at[c], (v, relay_to))
+
     for c in range(2):
         y_stage(xo, wyf, to_ratio, 8 * c, 8 * c + 8)
 
-        @pl.when(upper)
+        @pl.when(cross)
+        def _():
+            to_relay(c).start()
+            far_ratio(c).start()
+
+        @pl.when(near_hi)
         def _():
             up_ratio(c).start()
 
-        @pl.when(lower)
+        @pl.when(near_lo)
         def _():
             dn_ratio(c).start()
 
@@ -332,13 +390,23 @@
 
     for c in range(2):
 
-        @pl.when(lower)
+        @pl.when(relays)
+        def _():
+            to_relay(c).wait_recv()
+            from_relay(c).start()
+
+        @pl.when(near_lo)
         def _():
             up_ratio(c).wait_recv()
 
-        @pl.when(upper)
+        @pl.when(near_hi)
         def _():
             dn_ratio(c).wait_recv()
+
+        @pl.when(cross)
+        def _():
+            far_ratio(c).wait_recv()
+            from_relay(c).wait_recv()
 
     z_stage(rat, wzb, thi, tlo)
     x_stage(thi, tlo, cxb, exb, xo)
@@ -347,11 +415,11 @@
         logs[z] = jnp.log(back)
 
     def share_x(c, i):
-        src = logs.at[pl.ds(4 * c, 4), pl.ds(pl.multiple_of(xs[i] * 16, 16), 16), :]
+        src = logs.at[pl.ds(4 * c, 4), pl.ds(pl.multiple_of(xs[i + 1] * 16, 16), 16), :]
         return remote(src, xin.at[i, pl.ds(4 * c, 4)], sx_send.at[c, i], sx_recv.at[c, i], (xpeer[i], s))
 
     def share_z(c, i):
-        j = lax.rem(zl + i + 1, GROUP)
+        j = zs[i + 1]
         src = zout.at[j, pl.ds(16 * c, 16), :]
         return remote(src, zin.at[i, pl.ds(16 * c, 16), :], sz_send.at[c, i], sz_recv.at[c, i], (zpeer[i], s))
 
@@ -388,39 +456,44 @@
     for c in range(4):
         final(c)
 
+    def drain(stream):
+        for i in range(3):
+            to_z(stream, i).wait_send()
+        for i in range(2):
+            for k in range(4):
+                to_x(stream, i, k, v).wait_send()
+                on_x(stream, i, k, v).wait_send()
+
+    drain(main)
     for i in range(3):
-        to_z(v, 16, i, zsend, main_recv).wait_send()
-        for k in range(4):
-            to_x(v, 16, k, i, xsend, main_recv).wait_send()
         for c in range(4):
             share_x(c, i).wait_send()
             share_z(c, i).wait_send()
 
     @pl.when(cross)
     def _():
+        drain(side)
         to_far().wait_send()
-        for i in range(3):
-            to_z(v, my_off, i, czsend, cross_recv).wait_send()
-            for k in range(4):
-                to_x(v, my_off, k, i, cxsend, cross_recv).wait_send()
+        for c in range(2):
+            far_ratio(c).wait_send()
+            to_relay(c).wait_send()
+
+    @pl.when(relays)
+    def _():
+        for c in range(2):
+            from_relay(c).wait_send()
 
     @pl.when(near_hi)
     def _():
         for k in range(16):
             to_up(v, k).wait_send()
+        for c in range(2):
+            up_ratio(c).wait_send()
 
     @pl.when(near_lo)
     def _():
         for k in range(16):
             to_dn(v, k).wait_send()
-
-    @pl.when(upper)
-    def _():
-        for c in range(2):
-            up_ratio(c).wait_send()
-
-    @pl.when(lower)
-    def _():
         for c in range(2):
             dn_ratio(c).wait_send()
 
@@ -451,6 +524,7 @@
         scratch_shapes=[
             pltpu.VMEM((64, 48, 512), F32),
             pltpu.VMEM((4, 64, 48, 128), F32),
+            pltpu.VMEM((2, 4, 32, 8, 128), F32),
             pltpu.VMEM((16, 64, 512), F32),
             pltpu.VMEM((64, 48, 512), BF16),
             pltpu.VMEM((64, 48, 512), BF16),
@@ -463,8 +537,9 @@
         + TABLES * 2
         + [DMA((1,))]
         + [DMA((16,))] * 4
-        + [DMA((3,)), DMA((4, 3)), DMA((16,)), DMA((16,)), DMA((1,)), DMA((3,)), DMA((4, 3))]
-        + [DMA((2,))] * 4
+        + [DMA((3,))] * 2
+        + [DMA((3,)), DMA((3,)), DMA((2, 4)), DMA((2, 4)), DMA((2, 4)), DMA((2, 4))] * 2
+        + [DMA((2,))] * 8
         + [DMA((4, 3))] * 4,
         compiler_params=pltpu.CompilerParams(
             collective_id=0, has_side_effects=True, vmem_limit_bytes=60 << 20

time: 150 us -> 127 us (0.85)
  Pallas kernels: 145 us -> 121 us
    pallas_call x1, Pallas kernels: 145 us -> 121 us  [local(): pl.pallas_call(kernel, out_shape=jax.ShapeDtypeStruct(estimate.shape, F32...]
where the time goes in v3:
time: 127 us
  Pallas kernels  121 us (95%)
  local copies, waits for them, and re-layouts  5.39 us (4%)
    pallas_call x1, Pallas kernels, local(): pl.pallas_call(kernel, out_shape=jax.ShapeDtypeStruct(estimate.shape, F32...  121 us
    unnamed x4, local copies, waits for them, and re-layouts  3.61 us

profile of v3, /device:TPU:25, one launch (start us, length us, event | category | flops | bytes accessed | tf_op | source)
XLA Modules:
  0.0 126.5 jit_solution(12692030258202981770)
XLA Ops:
  0.0 0.7 copy.14
  0.7 0.6 pad.10.pz
  1.3 0.7 copy.13
  1.9 0.6 pad.11.py
  2.5 0.7 copy.12
  3.2 0.6 pad.12.px
  3.8 121.1 %deconvolve.1 = f32[16,4,512]{2,1,0:T(4,128)} custom-call(f32[3,32]{1,0:T(4,128)} %pad.10.pz, f32[3,32]{1,0:T(4,128)} %pad.11.py, f32[3,32]{1,0:T(4,128)} %pad.12.px, f32[16,4,512]{2,1,0:T(4,128)} %est.1, f32[16,64,512]{2,1,0:T(8,128)} %bitcast.10), custom_call_target="tpu_custom_call" | custom-call | tf_op jit(solution)/shard_map/deconvolve/pallas_call | solution.py:519
  125.0 1.6 %copy.16 = f32[16,4,512]{2,1,0:T(4,128)} copy(f32[16,4,512]{2,1,0:T(4,128)} %deconvolve.1) | data formatting | bytes 262144

commit v4 on v3

--- a/solution.py
+++ b/solution.py
@@ -31,21 +31,21 @@
 
 def build_tables(pz, py, px, wz, wy, cx, ex, back):
     def tap_of(ref):
-        return lambda k: ref[k // 32, k % 32]
+        return lambda k: ref[0, k // TAPS, k % TAPS]
 
     row, col = iotas((48, 96))
     p = jnp.where(col < 48, col, col - 48)
     d = (row % 16) - p + 31 if back else p - (row % 16) - 1
-    code = jnp.where((d >= 0) & (d < TAPS), (row // 16) * 32 + d, -1)
-    hi, lo = split(pick(code, RANK * 32, tap_of(pz)))
+    code = jnp.where((d >= 0) & (d < TAPS), (row // 16) * TAPS + d, -1)
+    hi, lo = split(pick(code, RANK * TAPS, tap_of(pz)))
     wz[0:48, :] = hi
     wz[48:96, :] = jnp.where(col < 48, lo.astype(F32), 0.0).astype(BF16)
 
     row, col = iotas((64, 384))
     c = jnp.where(col < 192, col, col - 192)
     d = row - (c % 64) + HALF if back else (c % 64) - row + HALF
-    code = jnp.where((d >= 0) & (d < TAPS), (c // 64) * 32 + d, -1)
-    hi, lo = split(pick(code, RANK * 32, tap_of(py)))
+    code = jnp.where((d >= 0) & (d < TAPS), (c // 64) * TAPS + d, -1)
+    hi, lo = split(pick(code, RANK * TAPS, tap_of(py)))
     wy[0:64, :] = hi
     wy[64:128, :] = jnp.where(col < 192, lo.astype(F32), 0.0).astype(BF16)
 
@@ -55,7 +55,7 @@
     near = (d >= 0) & (d < TAPS)
     zero = jnp.zeros((128, 128), BF16)
     for r in range(RANK):
-        full = pick(ring, TAPS, lambda k: px[r, k])
+        full = pick(ring, TAPS, lambda k: px[0, r, k])
         for ref, keep in ((cx, near), (ex, jnp.logical_not(near))):
             hi, lo = split(jnp.where(keep, full, 0.0))
             ref[r, 0:128, 0:128] = hi
@@ -68,64 +68,67 @@
     return jnp.dot(a, b, preferred_element_type=F32)
 
 
-def z_stage(src, wz, thi, tlo, unroll=4):
-    def one(y, _):
-        hi, lo = split(jnp.concatenate([src[b, y] for b in range(4)], axis=1))
-        o = dot(wz[...], jnp.concatenate([hi, lo], axis=0))
-        hi, lo = split(o[:48] + o[48:])
-        thi[y] = hi
-        tlo[y] = lo
-        return 0
-
-    lax.fori_loop(0, 64, one, 0, unroll=unroll)
-
-
-def x_stage(thi, tlo, cx, ex, xo, rows=8):
-    m = rows * 16
+def z_rows(load, wz, thi, tlo, start, count):
+    for i in range(0, count, 2):
+        pair = []
+        for y in (start + i, start + i + 1):
+            hi, lo = split(load(y))
+            o = dot(wz[...], jnp.concatenate([hi, lo], axis=0))
+            pair.append(o[:48] + o[48:])
+        rows = pl.ds(pl.multiple_of((start + i) * 8, 16), 16)
+        for h in range(2):
+            for r in range(RANK):
+                top = 16 * r + 8 * h
+                hi, lo = split(jnp.concatenate([p[top : top + 8] for p in pair], axis=0))
+                thi[h, r, rows, :] = hi
+                tlo[h, r, rows, :] = lo
+
+
+def x_stage(thi, tlo, cx, ex, xo, h, m=512):
     low = lax.broadcasted_iota(jnp.int32, (m, 128), 1) < 64
 
     for r in range(RANK):
 
         def one(c, _):
-            ys = pl.ds(c * rows, rows)
-            hi = thi[ys, 16 * r : 16 * r + 16, :].reshape(m, 512)
-            lo = tlo[ys, 16 * r : 16 * r + 16, :].reshape(m, 512)
-            h = [hi[:, 128 * b : 128 * b + 128] for b in range(4)]
-            l = [lo[:, 128 * b : 128 * b + 128] for b in range(4)]
-            out = []
+            rows = pl.ds(pl.multiple_of(c * m, m), m)
+            dest = pl.ds(pl.multiple_of(r * 512 + c * m, m), m)
+
+            def lanes(ref, b):
+                return ref[h, r, rows, 128 * b : 128 * b + 128]
+
+            before = jnp.zeros((m, 128), F32)
             for b in range(4):
-                o = dot(jnp.concatenate([h[b], l[b]], axis=1), cx[r])
-                out.append(o[:, :128] + o[:, 128:])
-            for b in range(3):
-                ph = jnp.where(low, h[b + 1], h[b])
-                pll = jnp.where(low, l[b + 1], l[b])
-                o = dot(jnp.concatenate([ph, pll], axis=1), ex[r])
-                e = o[:, :128] + o[:, 128:]
-                out[b] = out[b] + jnp.where(low, 0.0, e)
-                out[b + 1] = out[b + 1] + jnp.where(low, e, 0.0)
-            rr = pl.ds(r * 1024 + c * m, m)
-            for b in range(4):
-                xo[b, rr, :] = out[b]
+                hi, lo = lanes(thi, b), lanes(tlo, b)
+                o = dot(jnp.concatenate([hi, lo], axis=1), cx[r])
+                after = jnp.zeros((m, 128), F32)
+                if b < 3:
+                    hi = jnp.where(low, lanes(thi, b + 1), hi)
+                    lo = jnp.where(low, lanes(tlo, b + 1), lo)
+                    e = dot(jnp.concatenate([hi, lo], axis=1), ex[r])
+                    after = e[:, :128] + e[:, 128:]
+                xo[h, b, dest, :] = o[:, :128] + o[:, 128:] + jnp.where(low, before, after)
+                before = after
             return 0
 
-        lax.fori_loop(0, 64 // rows, one, 0)
-
-
-def y_stage(xo, wy, finish, lo=0, hi=16):
+        lax.fori_loop(0, 512 // m, one, 0, unroll=1)
+
+
+def y_stage(xo, wy, finish, h, lo=0, hi=8):
     def one(z, _):
         planes = []
         for r in range(RANK):
-            parts = [xo[b, pl.ds(r * 1024 + z, 64, stride=16), :] for b in range(4)]
+            parts = [xo[h, b, pl.ds(r * 512 + z, 64, stride=8), :] for b in range(4)]
             planes.append(jnp.concatenate(parts, axis=1))
-        h, l = split(jnp.concatenate(planes, axis=0))
-        o = dot(wy[...], jnp.concatenate([h, l], axis=0))
-        finish(z, o[:64] + o[64:])
+        a, l = split(jnp.concatenate(planes, axis=0))
+        o = dot(wy[...], jnp.concatenate([a, l], axis=0))
+        finish(8 * h + z, o[:64] + o[64:])
         return 0
 
-    lax.fori_loop(lo, hi, one, 0)
+    lax.fori_loop(lo, hi, one, 0, unroll=4)
 
 
 SLABS, GROUP = 16, 4
+DIRECT, PIECE = 36, 14
 MESH = pl.DeviceIdType.MESH
 
 
@@ -135,26 +138,16 @@
     )
 
 
-def z_rows(src, wz, thi, tlo, start, count):
-    for i in range(count):
-        y = start + i
-        hi, lo = split(src[y])
-        o = dot(wz[...], jnp.concatenate([hi, lo], axis=0))
-        hi, lo = split(o[:48] + o[48:])
-        thi[y] = hi
-        tlo[y] = lo
-
-
 def kernel(
     pz, py, px, est, obs_hbm, out,
-    fld, rat, relay, obs, thi, tlo, xo, logs, xin, zout, zin,
+    fld, rat, relay, obs, thi, tlo, xo, logs, pin, xin, zout, zin,
     wzf, wyf, cxf, exf, wzb, wyb, cxb, exb,
     obs_sem, lo_recv, hi_recv, upsend, dnsend, far_send, far_recv,
     mz_send, mz_recv, mx_send, mx_recv, mc_send, mc_recv,
     cz_send, cz_recv, cx_send, cx_recv, cc_send, cc_recv,
     rup_send, rdn_send, rlo_recv, rhi_recv,
     rel_send, rel_recv, fwd_send, fwd_recv,
-    sx_send, sx_recv, sz_send, sz_recv,
+    sp_send, sp_recv, sx_send, sx_recv, sz_send, sz_recv,
 ):
     v, s = lax.axis_index("view"), lax.axis_index("slab")
     x, zl = lax.div(v, GROUP), lax.rem(v, GROUP)
@@ -300,7 +293,7 @@
 
         def one(j, _):
             first = lax.rem(xs[0] + j, GROUP) * GROUP + zs[k]
-            z_rows(fld, wzf, thi, tlo, first * 4, 4)
+            z_rows(lambda y: fld[y], wzf, thi, tlo, first * 4, 4)
             return 0
 
         lax.fori_loop(0, GROUP, one, 0)
@@ -339,7 +332,6 @@
     z_group(2)
     z_group(3)
 
-    x_stage(thi, tlo, cxf, exf, xo)
     load.wait()
 
     def to_ratio(z, blurred):
@@ -356,26 +348,29 @@
         src, dst = (rat.at[:, :, pl.ds(o + 8 * c, 8), :] for o in (16, 32))
         return remote(src, dst, rdn_send.at[c], rhi_recv.at[c], (v, s - 1))
 
-    def rows_of(off, c, h):
-        return rat.at[:, pl.ds(32 * h, 32), pl.ds(pl.multiple_of(off + 8 * c, 8), 8), :]
+    def rows_of(off, c, first, count):
+        return rat.at[:, pl.ds(first, count), pl.ds(pl.multiple_of(off + 8 * c, 8), 8), :]
 
     def far_ratio(c):
-        src, dst = rows_of(16, c, 0), rows_of(far_off, c, 0)
+        src, dst = rows_of(16, c, 0, DIRECT), rows_of(far_off, c, 0, DIRECT)
         return remote(src, dst, far_send.at[1 + c], far_recv.at[1 + c], (v, far_slab))
 
-    def to_relay(c):
-        return remote(rows_of(16, c, 1), relay.at[c], rel_send.at[c], rel_recv.at[c], (v, my_relay))
-
-    def from_relay(c):
-        dst = rows_of(jnp.where(bottom, 0, 32), c, 1)
-        return remote(relay.at[c], dst, fwd_send.at[c], fwd_recv.at[c], (v, relay_to))
+    def to_relay(c, p):
+        src = rows_of(16, c, DIRECT + PIECE * p, PIECE)
+        return remote(src, relay.at[c, p], rel_send.at[c, p], rel_recv.at[c, p], (v, my_relay))
+
+    def from_relay(c, p):
+        dst = rows_of(jnp.where(bottom, 0, 32), c, DIRECT + PIECE * p, PIECE)
+        return remote(relay.at[c, p], dst, fwd_send.at[c, p], fwd_recv.at[c, p], (v, relay_to))
 
     for c in range(2):
-        y_stage(xo, wyf, to_ratio, 8 * c, 8 * c + 8)
+        x_stage(thi, tlo, cxf, exf, xo, c)
+        y_stage(xo, wyf, to_ratio, c)
 
         @pl.when(cross)
         def _():
-            to_relay(c).start()
+            to_relay(c, 0).start()
+            to_relay(c, 1).start()
             far_ratio(c).start()
 
         @pl.when(near_hi)
@@ -392,8 +387,9 @@
 
         @pl.when(relays)
         def _():
-            to_relay(c).wait_recv()
-            from_relay(c).start()
+            for p in range(2):
+                to_relay(c, p).wait_recv()
+                from_relay(c, p).start()
 
         @pl.when(near_lo)
         def _():
@@ -406,30 +402,58 @@
         @pl.when(cross)
         def _():
             far_ratio(c).wait_recv()
-            from_relay(c).wait_recv()
-
-    z_stage(rat, wzb, thi, tlo)
-    x_stage(thi, tlo, cxb, exb, xo)
+            for p in range(2):
+                from_relay(c, p).wait_recv()
+
+    def ratio_rows(y):
+        return jnp.concatenate([rat[b, y] for b in range(4)], axis=1)
+
+    def z_back(n, _):
+        z_rows(ratio_rows, wzb, thi, tlo, n * 16, 16)
+        return 0
+
+    lax.fori_loop(0, 64 // 16, z_back, 0)
 
     def to_log(z, back):
         logs[z] = jnp.log(back)
 
+    def x_rows(j, c, first, count):
+        start = pl.multiple_of(xs[j] * 16 + first, 8)
+        return logs.at[pl.ds(4 * c, 4), pl.ds(start, count), :]
+
+    def share_far(c, i):
+        dst = pin.at[i, pl.ds(4 * c, 4)]
+        return remote(x_rows(3, c, 8 - 8 * i, 8), dst, sp_send.at[c, i], sp_recv.at[c, i], (xpeer[i], s))
+
     def share_x(c, i):
-        src = logs.at[pl.ds(4 * c, 4), pl.ds(pl.multiple_of(xs[i + 1] * 16, 16), 16), :]
-        return remote(src, xin.at[i, pl.ds(4 * c, 4)], sx_send.at[c, i], sx_recv.at[c, i], (xpeer[i], s))
+        dst = xin.at[i, pl.ds(4 * c, 4)]
+        return remote(x_rows(1 + i, c, 0, 16), dst, sx_send.at[c, i], sx_recv.at[c, i], (xpeer[i], s))
 
     def share_z(c, i):
         j = zs[i + 1]
         src = zout.at[j, pl.ds(16 * c, 16), :]
         return remote(src, zin.at[i, pl.ds(16 * c, 16), :], sz_send.at[c, i], sz_recv.at[c, i], (zpeer[i], s))
 
+    def send_far(c):
+        for i in range(2):
+            share_far(c, i).start()
+
+    def send_near(c):
+        for i in range(2):
+            share_far(c, i).wait_recv()
+            j, first = 2 - i, 8 - 8 * i
+            ref = x_rows(j, c, first, 8)
+            ref[...] = ref[...] + pin[i, 4 * c : 4 * c + 4]
+        for i in range(2):
+            share_x(c, i).start()
+
     def reduce_x(c):
-        for i in range(3):
+        for i in range(2):
             share_x(c, i).wait_recv()
         for q in range(4):
             z = 4 * c + q
             total = logs[z, pl.ds(pl.multiple_of(x * 16, 16), 16), :]
-            for i in range(3):
+            for i in range(2):
                 total = total + xin[i, z]
             for j in range(4):
                 zout[j, 4 * z : 4 * z + 4, :] = total[4 * j : 4 * j + 4]
@@ -445,13 +469,24 @@
             total = zout[zl, rows, :]
             for i in range(3):
                 total = total + zin[i, rows, :]
-            out[z] = est[z] * jnp.exp(total)
-
-    for c in range(4):
-        y_stage(xo, wyb, to_log, 4 * c, 4 * c + 4)
-        for i in range(3):
-            share_x(c, i).start()
-    for c in range(4):
+            out[z] = total
+
+    x_stage(thi, tlo, cxb, exb, xo, 0)
+    y_stage(xo, wyb, to_log, 0, 0, 4)
+    send_far(0)
+    y_stage(xo, wyb, to_log, 0, 4, 8)
+    send_far(1)
+    x_stage(thi, tlo, cxb, exb, xo, 1)
+    send_near(0)
+    y_stage(xo, wyb, to_log, 1, 0, 4)
+    send_far(2)
+    send_near(1)
+    y_stage(xo, wyb, to_log, 1, 4, 8)
+    send_far(3)
+    send_near(2)
+    reduce_x(0)
+    send_near(3)
+    for c in range(1, 4):
         reduce_x(c)
     for c in range(4):
         final(c)
@@ -465,9 +500,11 @@
                 on_x(stream, i, k, v).wait_send()
 
     drain(main)
-    for i in range(3):
-        for c in range(4):
+    for c in range(4):
+        for i in range(2):
+            share_far(c, i).wait_send()
             share_x(c, i).wait_send()
+        for i in range(3):
             share_z(c, i).wait_send()
 
     @pl.when(cross)
@@ -476,12 +513,14 @@
         to_far().wait_send()
         for c in range(2):
             far_ratio(c).wait_send()
-            to_relay(c).wait_send()
+            to_relay(c, 0).wait_send()
+            to_relay(c, 1).wait_send()
 
     @pl.when(relays)
     def _():
         for c in range(2):
-            from_relay(c).wait_send()
+            from_relay(c, 0).wait_send()
+            from_relay(c, 1).wait_send()
 
     @pl.when(near_hi)
     def _():
@@ -510,13 +549,8 @@
 ANY = pl.BlockSpec(memory_space=pl.ANY)
 
 
-def padded(taps):
-    return jnp.pad(taps, ((0, 0), (0, 1)))
-
-
 def local(estimate, observed, psf_z, psf_y, psf_x):
-    pz, py, px = (padded(t[0]) for t in (psf_z, psf_y, psf_x))
-    return pl.pallas_call(
+    share = pl.pallas_call(
         kernel,
         out_shape=jax.ShapeDtypeStruct(estimate.shape, F32),
         in_specs=[SMEM] * 3 + [VM, ANY],
@@ -524,13 +558,14 @@
         scratch_shapes=[
             pltpu.VMEM((64, 48, 512), F32),
             pltpu.VMEM((4, 64, 48, 128), F32),
-            pltpu.VMEM((2, 4, 32, 8, 128), F32),
+            pltpu.VMEM((2, 2, 4, PIECE, 8, 128), F32),
             pltpu.VMEM((16, 64, 512), F32),
-            pltpu.VMEM((64, 48, 512), BF16),
-            pltpu.VMEM((64, 48, 512), BF16),
-            pltpu.VMEM((4, 3072, 128), F32),
+            pltpu.VMEM((2, 3, 512, 512), BF16),
+            pltpu.VMEM((2, 3, 512, 512), BF16),
+            pltpu.VMEM((2, 4, 1536, 128), F32),
             pltpu.VMEM((16, 64, 512), F32),
-            pltpu.VMEM((3, 16, 16, 512), F32),
+            pltpu.VMEM((2, 16, 8, 512), F32),
+            pltpu.VMEM((2, 16, 16, 512), F32),
             pltpu.VMEM((4, 64, 512), F32),
             pltpu.VMEM((3, 64, 512), F32),
         ]
@@ -539,13 +574,16 @@
         + [DMA((16,))] * 4
         + [DMA((3,))] * 2
         + [DMA((3,)), DMA((3,)), DMA((2, 4)), DMA((2, 4)), DMA((2, 4)), DMA((2, 4))] * 2
-        + [DMA((2,))] * 8
-        + [DMA((4, 3))] * 4,
+        + [DMA((2,))] * 4
+        + [DMA((2, 2))] * 4
+        + [DMA((4, 2))] * 4
+        + [DMA((4, 3))] * 2,
         compiler_params=pltpu.CompilerParams(
             collective_id=0, has_side_effects=True, vmem_limit_bytes=60 << 20
         ),
         name="deconvolve",
-    )(pz, py, px, estimate, observed[0])
+    )(psf_z, psf_y, psf_x, estimate, observed[0])
+    return estimate * jnp.exp(share)
 
 
 def solution(mesh):

time: 127 us -> 109 us (0.86)
  Pallas kernels: 121 us -> 103 us
  other arithmetic: 0 us -> 1.59 us
  local copies, waits for them, and re-layouts: 5.39 us -> 3.81 us
    pallas_call x1, Pallas kernels: 121 us -> 103 us  [local(): pl.pallas_call(kernel, out_shape=jax.ShapeDtypeStruct(estimate.shape, F32...]
    pad x3 -> x0, local copies, waits for them, and re-layouts: 1.78 us -> none  [padded(): return jnp.pad(taps, ((0, 0), (0, 1)))]
    mul x0 -> x1, other arithmetic: none -> 1.59 us  [local(): return estimate * jnp.exp(share)]
    unnamed x4 -> x5, local copies, waits for them, and re-layouts: 3.61 us -> 3.81 us
where the time goes in v4:
time: 109 us; the launch traced here: 108 us
  Pallas kernels  103 us (94%)
  local copies, waits for them, and re-layouts  3.81 us (3%)
  other arithmetic  1.59 us (1%)
    pallas_call x1, Pallas kernels, local(): pl.pallas_call(kernel, out_shape=jax.ShapeDtypeStruct(estimate.shape, F32...  103 us
    unnamed x5, local copies, waits for them, and re-layouts  3.81 us

profile of v4, /device:TPU:25, one launch (start us, length us, event | category | flops | bytes accessed | tf_op | source)
XLA Modules:
  0.0 108.5 jit_solution(8479457131874506842)
XLA Ops:
  0.0 0.0 copy-start
  0.0 1.3 %copy.6.pz = f32[1,3,31]{2,1,0:T(4,128)} copy(f32[1,3,31]{2,0,1:T(1,128)} %param.7) | data formatting | bytes 744 | tf_op args[2]
  1.3 1.3 %copy.7.py = f32[1,3,31]{2,1,0:T(4,128)} copy(f32[1,3,31]{2,0,1:T(1,128)} %param.8) | data formatting | bytes 744 | tf_op args[3]
  2.6 1.2 %copy.8.px = f32[1,3,31]{2,1,0:T(4,128)} copy(f32[1,3,31]{2,0,1:T(1,128)} %param.9) | data formatting | bytes 744 | tf_op args[4]
  3.8 103.0 %deconvolve.1 = f32[16,4,512]{2,1,0:T(4,128)} custom-call(f32[1,3,31]{2,1,0:T(4,128)} %copy.6.pz, f32[1,3,31]{2,1,0:T(4,128)} %copy.7.py, f32[1,3,31]{2,1,0:T(4,128)} %copy.8.px, f32[16,4,512]{2,1,0:T(4,128)} %est.1, f32[16,64,512]{2,1,0:T(8,128)} %bitcast.4), custom_call_target="tpu_custom_call" | custom-call | tf_op jit(solution)/shard_map/deconvolve/pallas_call | solution.py:553
  106.9 0.0 copy-done
  106.9 1.6 %exponential_multiply_fusion = f32[8,8,512]{2,1,0:T(8,128)} fusion(f32[8,8,512]{2,1,0:T(8,128)S(1)} %bitcast.5, f32[8,8,512]{2,1,0:T(8,128)} %bitcast.6), kind=kLoop, calls=%fused_computation | loop fusion | flops 32768 | bytes 393216 | tf_op jit(solution)/shard_map/mul | solution.py:586
Async XLA Ops:
  0.0 106.9 %copy-start = (f32[16,4,512]{2,1,0:T(4,128)S(1)}, f32[16,4,512]{2,1,0:T(4,128)}, u32[]{:S(2)}) copy-start(f32[16,4,512]{2,1,0:T(4,128)} %est.1) | copy-start | bytes 393220

commit v5 on v4

--- a/solution.py
+++ b/solution.py
@@ -31,7 +31,7 @@
 
 def build_tables(pz, py, px, wz, wy, cx, ex, back):
     def tap_of(ref):
-        return lambda k: ref[0, k // TAPS, k % TAPS]
+        return lambda k: ref[k // TAPS, 0, k % TAPS]
 
     row, col = iotas((48, 96))
     p = jnp.where(col < 48, col, col - 48)
@@ -55,7 +55,7 @@
     near = (d >= 0) & (d < TAPS)
     zero = jnp.zeros((128, 128), BF16)
     for r in range(RANK):
-        full = pick(ring, TAPS, lambda k: px[0, r, k])
+        full = pick(ring, TAPS, lambda k: px[r, 0, k])
         for ref, keep in ((cx, near), (ex, jnp.logical_not(near))):
             hi, lo = split(jnp.where(keep, full, 0.0))
             ref[r, 0:128, 0:128] = hi
@@ -128,7 +128,7 @@
 
 
 SLABS, GROUP = 16, 4
-DIRECT, PIECE = 36, 14
+DIRECT, PIECE = 34, 15
 MESH = pl.DeviceIdType.MESH
 
 
@@ -306,8 +306,6 @@
 
     take_near(main, 1)
     take_x(main, 0)
-    take_near(main, 2)
-    take_near(main, 3)
 
     @pl.when(cross)
     def _():
@@ -316,19 +314,24 @@
             to_z(side, i).start()
         take_near(side, 0)
 
+    take_x(main, 1)
+    crossing((take_near, 1))
+    take_near(main, 2)
+    take_near(main, 3)
+    crossing((take_x, 0))
     take_far(main, 0)
-    take_x(main, 1)
-    crossing((take_near, 1), (take_x, 0))
+    crossing((take_x, 1), (take_near, 2), (take_near, 3))
     take_far(main, 1)
     take_x(main, 2)
-    crossing((take_near, 2), (take_near, 3), (take_far, 0), (take_x, 1))
-    z_group(0)
-    take_far(main, 2)
+    crossing((take_far, 0))
     take_x(main, 3)
     crossing((take_x, 2), (take_far, 1))
+    take_far(main, 2)
+    crossing((take_x, 3))
+    z_group(0)
     z_group(1)
     take_far(main, 3)
-    crossing((take_x, 3), (take_far, 2), (take_far, 3))
+    crossing((take_far, 2), (take_far, 3))
     z_group(2)
     z_group(3)
 
@@ -550,6 +553,7 @@
 
 
 def local(estimate, observed, psf_z, psf_y, psf_x):
+    taps = [jnp.swapaxes(p, 0, 1) for p in (psf_z, psf_y, psf_x)]
     share = pl.pallas_call(
         kernel,
         out_shape=jax.ShapeDtypeStruct(estimate.shape, F32),
@@ -582,7 +586,7 @@
             collective_id=0, has_side_effects=True, vmem_limit_bytes=60 << 20
         ),
         name="deconvolve",
-    )(psf_z, psf_y, psf_x, estimate, observed[0])
+    )(*taps, estimate, observed[0])
     return estimate * jnp.exp(share)
 
 

time: 109 us -> 105 us (0.963)
  local copies, waits for them, and re-layouts: 3.81 us -> 0.01 us
    unnamed x5 -> x2, local copies, waits for them, and re-layouts: 3.81 us -> 0.01 us
where the time goes in v5:
time: 105 us; the launch traced here: 104 us
  Pallas kernels  103 us (98%)
  other arithmetic  1.59 us (2%)
    pallas_call x1, Pallas kernels, local(): pl.pallas_call(kernel, out_shape=jax.ShapeDtypeStruct(estimate.shape, F32...  103 us

profile of v5, /device:TPU:25, one launch (start us, length us, event | category | flops | bytes accessed | tf_op | source)
XLA Modules:
  0.0 104.4 jit_solution(13095760384706286774)
XLA Ops:
  0.0 0.0 copy-start
  0.0 102.8 %deconvolve.1 = f32[16,4,512]{2,1,0:T(4,128)} custom-call(f32[3,1,31]{2,1,0:T(1,128)} %bitcast.10, f32[3,1,31]{2,1,0:T(1,128)} %bitcast.11, f32[3,1,31]{2,1,0:T(1,128)} %bitcast.12, f32[16,4,512]{2,1,0:T(4,128)} %est.1, f32[16,64,512]{2,1,0:T(8,128)} %bitcast.7), custom_call_target="tpu_custom_call" | custom-call | tf_op jit(solution)/shard_map/deconvolve/pallas_call | solution.py:557
  102.8 0.0 copy-done
  102.8 1.6 %exponential_multiply_fusion = f32[8,8,512]{2,1,0:T(8,128)} fusion(f32[8,8,512]{2,1,0:T(8,128)S(1)} %bitcast.8, f32[8,8,512]{2,1,0:T(8,128)} %bitcast.9), kind=kLoop, calls=%fused_computation | loop fusion | flops 32768 | bytes 393216 | tf_op jit(solution)/shard_map/mul | solution.py:590
Async XLA Ops:
  0.0 102.8 %copy-start = (f32[16,4,512]{2,1,0:T(4,128)S(1)}, f32[16,4,512]{2,1,0:T(4,128)}, u32[]{:S(2)}) copy-start(f32[16,4,512]{2,1,0:T(4,128)} %est.1) | copy-start | bytes 393220

commit v6 on v5

--- a/solution.py
+++ b/solution.py
@@ -84,14 +84,14 @@
                 tlo[h, r, rows, :] = lo
 
 
-def x_stage(thi, tlo, cx, ex, xo, h, m=512):
+def x_stage(thi, tlo, cx, ex, xo, h, first=0, m=512):
     low = lax.broadcasted_iota(jnp.int32, (m, 128), 1) < 64
 
     for r in range(RANK):
 
-        def one(c, _):
-            rows = pl.ds(pl.multiple_of(c * m, m), m)
-            dest = pl.ds(pl.multiple_of(r * 512 + c * m, m), m)
+        def one():
+            rows = pl.ds(first, m)
+            dest = pl.ds(r * 512 + first, m)
 
             def lanes(ref, b):
                 return ref[h, r, rows, 128 * b : 128 * b + 128]
@@ -108,9 +108,8 @@
                     after = e[:, :128] + e[:, 128:]
                 xo[h, b, dest, :] = o[:, :128] + o[:, 128:] + jnp.where(low, before, after)
                 before = after
-            return 0
-
-        lax.fori_loop(0, 512 // m, one, 0, unroll=1)
+
+        one()
 
 
 def y_stage(xo, wy, finish, h, lo=0, hi=8):
@@ -128,7 +127,9 @@
 
 
 SLABS, GROUP = 16, 4
-DIRECT, PIECE = 34, 15
+DIRECT, PIECE = 32, 16
+CHUNKS, DEEP = 8, 2
+PARTS = ((0, 0, 64), (1, 0, 32), (1, 32, 32))
 MESH = pl.DeviceIdType.MESH
 
 
@@ -343,13 +344,16 @@
             rows = rat.at[b].reshape(3072, 128)
             rows[pl.ds(z + 16, 64, stride=48), :] = ratio[:, 128 * b : 128 * b + 128]
 
-    def up_ratio(c):
-        src, dst = (rat.at[:, :, pl.ds(o + 8 * c, 8), :] for o in (16, 0))
-        return remote(src, dst, rup_send.at[c], rlo_recv.at[c], (v, s + 1))
-
-    def dn_ratio(c):
-        src, dst = (rat.at[:, :, pl.ds(o + 8 * c, 8), :] for o in (16, 32))
-        return remote(src, dst, rdn_send.at[c], rhi_recv.at[c], (v, s - 1))
+    def slab_ratio(n, off, send, recv, slab):
+        c, first, count = PARTS[n]
+        src, dst = (rat.at[:, pl.ds(first, count), pl.ds(o + 8 * c, 8), :] for o in (16, off))
+        return remote(src, dst, send.at[n], recv.at[n], (v, slab))
+
+    def up_ratio(n):
+        return slab_ratio(n, 0, rup_send, rlo_recv, s + 1)
+
+    def dn_ratio(n):
+        return slab_ratio(n, 32, rdn_send, rhi_recv, s - 1)
 
     def rows_of(off, c, first, count):
         return rat.at[:, pl.ds(first, count), pl.ds(pl.multiple_of(off + 8 * c, 8), 8), :]
@@ -378,35 +382,33 @@
 
         @pl.when(near_hi)
         def _():
-            up_ratio(c).start()
+            for n in (0,) if c == 0 else (1, 2):
+                up_ratio(n).start()
 
         @pl.when(near_lo)
         def _():
-            dn_ratio(c).start()
+            for n in (0,) if c == 0 else (1, 2):
+                dn_ratio(n).start()
 
     build_tables(pz, py, px, wzb, wyb, cxb, exb, True)
 
-    for c in range(2):
-
-        @pl.when(relays)
-        def _():
+    @pl.when(relays)
+    def _():
+        for c in range(2):
             for p in range(2):
                 to_relay(c, p).wait_recv()
                 from_relay(c, p).start()
 
+    def take_ratio(parts):
         @pl.when(near_lo)
         def _():
-            up_ratio(c).wait_recv()
+            for n in parts:
+                up_ratio(n).wait_recv()
 
         @pl.when(near_hi)
         def _():
-            dn_ratio(c).wait_recv()
-
-        @pl.when(cross)
-        def _():
-            far_ratio(c).wait_recv()
-            for p in range(2):
-                from_relay(c, p).wait_recv()
+            for n in parts:
+                dn_ratio(n).wait_recv()
 
     def ratio_rows(y):
         return jnp.concatenate([rat[b, y] for b in range(4)], axis=1)
@@ -415,27 +417,46 @@
         z_rows(ratio_rows, wzb, thi, tlo, n * 16, 16)
         return 0
 
-    lax.fori_loop(0, 64 // 16, z_back, 0)
+    take_ratio((0, 1))
+
+    @pl.when(cross)
+    def _():
+        for c in range(2):
+            far_ratio(c).wait_recv()
+        for p in range(2):
+            from_relay(0, p).wait_recv()
+
+    lax.fori_loop(0, 2, z_back, 0)
+    for h in range(2):
+        x_stage(thi, tlo, cxb, exb, xo, h, 0, 256)
+    take_ratio((2,))
+
+    @pl.when(cross)
+    def _():
+        for p in range(2):
+            from_relay(1, p).wait_recv()
+
+    lax.fori_loop(2, 4, z_back, 0)
 
     def to_log(z, back):
         logs[z] = jnp.log(back)
 
     def x_rows(j, c, first, count):
         start = pl.multiple_of(xs[j] * 16 + first, 8)
-        return logs.at[pl.ds(4 * c, 4), pl.ds(start, count), :]
+        return logs.at[pl.ds(DEEP * c, DEEP), pl.ds(start, count), :]
 
     def share_far(c, i):
-        dst = pin.at[i, pl.ds(4 * c, 4)]
+        dst = pin.at[i, pl.ds(DEEP * c, DEEP)]
         return remote(x_rows(3, c, 8 - 8 * i, 8), dst, sp_send.at[c, i], sp_recv.at[c, i], (xpeer[i], s))
 
     def share_x(c, i):
-        dst = xin.at[i, pl.ds(4 * c, 4)]
+        dst = xin.at[i, pl.ds(DEEP * c, DEEP)]
         return remote(x_rows(1 + i, c, 0, 16), dst, sx_send.at[c, i], sx_recv.at[c, i], (xpeer[i], s))
 
     def share_z(c, i):
         j = zs[i + 1]
-        src = zout.at[j, pl.ds(16 * c, 16), :]
-        return remote(src, zin.at[i, pl.ds(16 * c, 16), :], sz_send.at[c, i], sz_recv.at[c, i], (zpeer[i], s))
+        src = zout.at[j, pl.ds(4 * DEEP * c, 4 * DEEP), :]
+        return remote(src, zin.at[i, pl.ds(4 * DEEP * c, 4 * DEEP), :], sz_send.at[c, i], sz_recv.at[c, i], (zpeer[i], s))
 
     def send_far(c):
         for i in range(2):
@@ -446,15 +467,15 @@
             share_far(c, i).wait_recv()
             j, first = 2 - i, 8 - 8 * i
             ref = x_rows(j, c, first, 8)
-            ref[...] = ref[...] + pin[i, 4 * c : 4 * c + 4]
+            ref[...] = ref[...] + pin[i, DEEP * c : DEEP * c + DEEP]
         for i in range(2):
             share_x(c, i).start()
 
     def reduce_x(c):
         for i in range(2):
             share_x(c, i).wait_recv()
-        for q in range(4):
-            z = 4 * c + q
+        for q in range(DEEP):
+            z = DEEP * c + q
             total = logs[z, pl.ds(pl.multiple_of(x * 16, 16), 16), :]
             for i in range(2):
                 total = total + xin[i, z]
@@ -466,32 +487,38 @@
     def final(c):
         for i in range(3):
             share_z(c, i).wait_recv()
-        for q in range(4):
-            z = 4 * c + q
+        for q in range(DEEP):
+            z = DEEP * c + q
             rows = pl.ds(4 * z, 4)
             total = zout[zl, rows, :]
             for i in range(3):
                 total = total + zin[i, rows, :]
             out[z] = total
 
-    x_stage(thi, tlo, cxb, exb, xo, 0)
+    x_stage(thi, tlo, cxb, exb, xo, 0, 256, 256)
     y_stage(xo, wyb, to_log, 0, 0, 4)
     send_far(0)
+    send_far(1)
     y_stage(xo, wyb, to_log, 0, 4, 8)
-    send_far(1)
-    x_stage(thi, tlo, cxb, exb, xo, 1)
+    send_far(2)
+    send_far(3)
+    x_stage(thi, tlo, cxb, exb, xo, 1, 256, 256)
     send_near(0)
+    send_near(1)
     y_stage(xo, wyb, to_log, 1, 0, 4)
-    send_far(2)
-    send_near(1)
+    send_far(4)
+    send_far(5)
+    send_near(2)
+    send_near(3)
     y_stage(xo, wyb, to_log, 1, 4, 8)
-    send_far(3)
-    send_near(2)
-    reduce_x(0)
-    send_near(3)
-    for c in range(1, 4):
+    send_far(6)
+    send_far(7)
+    for c in range(4, CHUNKS):
+        send_near(c)
+        reduce_x(c - 4)
+    for c in range(4, CHUNKS):
         reduce_x(c)
-    for c in range(4):
+    for c in range(CHUNKS):
         final(c)
 
     def drain(stream):
@@ -503,7 +530,7 @@
                 on_x(stream, i, k, v).wait_send()
 
     drain(main)
-    for c in range(4):
+    for c in range(CHUNKS):
         for i in range(2):
             share_far(c, i).wait_send()
             share_x(c, i).wait_send()
@@ -529,15 +556,15 @@
     def _():
         for k in range(16):
             to_up(v, k).wait_send()
-        for c in range(2):
-            up_ratio(c).wait_send()
+        for n in range(3):
+            up_ratio(n).wait_send()
 
     @pl.when(near_lo)
     def _():
         for k in range(16):
             to_dn(v, k).wait_send()
-        for c in range(2):
-            dn_ratio(c).wait_send()
+        for n in range(3):
+            dn_ratio(n).wait_send()
 
 
 TABLES = [
@@ -578,10 +605,10 @@
         + [DMA((16,))] * 4
         + [DMA((3,))] * 2
         + [DMA((3,)), DMA((3,)), DMA((2, 4)), DMA((2, 4)), DMA((2, 4)), DMA((2, 4))] * 2
-        + [DMA((2,))] * 4
+        + [DMA((3,))] * 4
         + [DMA((2, 2))] * 4
-        + [DMA((4, 2))] * 4
-        + [DMA((4, 3))] * 2,
+        + [DMA((CHUNKS, 2))] * 4
+        + [DMA((CHUNKS, 3))] * 2,
         compiler_params=pltpu.CompilerParams(
             collective_id=0, has_side_effects=True, vmem_limit_bytes=60 << 20
         ),

time: 105 us -> 102 us (0.971)
  Pallas kernels: 103 us -> 101 us
    pallas_call x1, Pallas kernels: 103 us -> 101 us  [local(): pl.pallas_call(kernel, out_shape=jax.ShapeDtypeStruct(estimate.shape, F32...]
where the time goes in v6:
time: 102 us
  Pallas kernels  101 us (99%)
  other arithmetic  1.59 us (2%)
    pallas_call x1, Pallas kernels, local(): pl.pallas_call(kernel, out_shape=jax.ShapeDtypeStruct(estimate.shape, F32...  101 us

profile of v6, /device:TPU:25, one launch (start us, length us, event | category | flops | bytes accessed | tf_op | source)
XLA Modules:
  0.0 102.4 jit_solution(2309309903509423749)
XLA Ops:
  0.0 0.0 copy-start
  0.0 100.8 %deconvolve.1 = f32[16,4,512]{2,1,0:T(4,128)} custom-call(f32[3,1,31]{2,1,0:T(1,128)} %bitcast.10, f32[3,1,31]{2,1,0:T(1,128)} %bitcast.11, f32[3,1,31]{2,1,0:T(1,128)} %bitcast.12, f32[16,4,512]{2,1,0:T(4,128)} %est.1, f32[16,64,512]{2,1,0:T(8,128)} %bitcast.7), custom_call_target="tpu_custom_call" | custom-call | tf_op jit(solution)/shard_map/deconvolve/pallas_call | solution.py:584
  100.8 0.0 copy-done
  100.8 1.6 %exponential_multiply_fusion = f32[8,8,512]{2,1,0:T(8,128)} fusion(f32[8,8,512]{2,1,0:T(8,128)S(1)} %bitcast.8, f32[8,8,512]{2,1,0:T(8,128)} %bitcast.9), kind=kLoop, calls=%fused_computation | loop fusion | flops 32768 | bytes 393216 | tf_op jit(solution)/shard_map/mul | solution.py:617
Async XLA Ops:
  0.0 100.8 %copy-start = (f32[16,4,512]{2,1,0:T(4,128)S(1)}, f32[16,4,512]{2,1,0:T(4,128)}, u32[]{:S(2)}) copy-start(f32[16,4,512]{2,1,0:T(4,128)} %est.1) | copy-start | bytes 393220

commit v7 on v6

--- a/solution.py
+++ b/solution.py
@@ -127,7 +127,7 @@
 
 
 SLABS, GROUP = 16, 4
-DIRECT, PIECE = 32, 16
+DIRECT, PIECE, PIECES = 32, 8, 4
 CHUNKS, DEEP = 8, 2
 PARTS = ((0, 0, 64), (1, 0, 32), (1, 32, 32))
 MESH = pl.DeviceIdType.MESH
@@ -330,10 +330,11 @@
     take_far(main, 2)
     crossing((take_x, 3))
     z_group(0)
+    take_far(main, 3)
     z_group(1)
-    take_far(main, 3)
-    crossing((take_far, 2), (take_far, 3))
+    crossing((take_far, 2))
     z_group(2)
+    crossing((take_far, 3))
     z_group(3)
 
     load.wait()
@@ -376,8 +377,8 @@
 
         @pl.when(cross)
         def _():
-            to_relay(c, 0).start()
-            to_relay(c, 1).start()
+            for p in range(PIECES):
+                to_relay(c, p).start()
             far_ratio(c).start()
 
         @pl.when(near_hi)
@@ -395,7 +396,7 @@
     @pl.when(relays)
     def _():
         for c in range(2):
-            for p in range(2):
+            for p in range(PIECES):
                 to_relay(c, p).wait_recv()
                 from_relay(c, p).start()
 
@@ -423,7 +424,7 @@
     def _():
         for c in range(2):
             far_ratio(c).wait_recv()
-        for p in range(2):
+        for p in range(PIECES):
             from_relay(0, p).wait_recv()
 
     lax.fori_loop(0, 2, z_back, 0)
@@ -433,7 +434,7 @@
 
     @pl.when(cross)
     def _():
-        for p in range(2):
+        for p in range(PIECES):
             from_relay(1, p).wait_recv()
 
     lax.fori_loop(2, 4, z_back, 0)
@@ -543,14 +544,14 @@
         to_far().wait_send()
         for c in range(2):
             far_ratio(c).wait_send()
-            to_relay(c, 0).wait_send()
-            to_relay(c, 1).wait_send()
+            for p in range(PIECES):
+                to_relay(c, p).wait_send()
 
     @pl.when(relays)
     def _():
         for c in range(2):
-            from_relay(c, 0).wait_send()
-            from_relay(c, 1).wait_send()
+            for p in range(PIECES):
+                from_relay(c, p).wait_send()
 
     @pl.when(near_hi)
     def _():
@@ -589,7 +590,7 @@
         scratch_shapes=[
             pltpu.VMEM((64, 48, 512), F32),
             pltpu.VMEM((4, 64, 48, 128), F32),
-            pltpu.VMEM((2, 2, 4, PIECE, 8, 128), F32),
+            pltpu.VMEM((2, PIECES, 4, PIECE, 8, 128), F32),
             pltpu.VMEM((16, 64, 512), F32),
             pltpu.VMEM((2, 3, 512, 512), BF16),
             pltpu.VMEM((2, 3, 512, 512), BF16),
@@ -606,7 +607,7 @@
         + [DMA((3,))] * 2
         + [DMA((3,)), DMA((3,)), DMA((2, 4)), DMA((2, 4)), DMA((2, 4)), DMA((2, 4))] * 2
         + [DMA((3,))] * 4
-        + [DMA((2, 2))] * 4
+        + [DMA((2, PIECES))] * 4
         + [DMA((CHUNKS, 2))] * 4
         + [DMA((CHUNKS, 3))] * 2,
         compiler_params=pltpu.CompilerParams(

time: 102 us -> 102 us (level)
  no operation moved by 1% of the time
where the time goes in v7:
time: 102 us
  Pallas kernels  100 us (98%)
  other arithmetic  1.59 us (2%)
    pallas_call x1, Pallas kernels, local(): pl.pallas_call(kernel, out_shape=jax.ShapeDtypeStruct(estimate.shape, F32...  100 us

profile of v7, /device:TPU:25, one launch (start us, length us, event | category | flops | bytes accessed | tf_op | source)
XLA Modules:
  0.0 101.9 jit_solution(7267243740039478223)
XLA Ops:
  0.0 0.0 copy-start
  0.0 100.3 %deconvolve.1 = f32[16,4,512]{2,1,0:T(4,128)} custom-call(f32[3,1,31]{2,1,0:T(1,128)} %bitcast.10, f32[3,1,31]{2,1,0:T(1,128)} %bitcast.11, f32[3,1,31]{2,1,0:T(1,128)} %bitcast.12, f32[16,4,512]{2,1,0:T(4,128)} %est.1, f32[16,64,512]{2,1,0:T(8,128)} %bitcast.7), custom_call_target="tpu_custom_call" | custom-call | tf_op jit(solution)/shard_map/deconvolve/pallas_call | solution.py:585
  100.3 0.0 copy-done
  100.3 1.6 %exponential_multiply_fusion = f32[8,8,512]{2,1,0:T(8,128)} fusion(f32[8,8,512]{2,1,0:T(8,128)S(1)} %bitcast.8, f32[8,8,512]{2,1,0:T(8,128)} %bitcast.9), kind=kLoop, calls=%fused_computation | loop fusion | flops 32768 | bytes 393216 | tf_op jit(solution)/shard_map/mul | solution.py:618
Async XLA Ops:
  0.0 100.3 %copy-start = (f32[16,4,512]{2,1,0:T(4,128)S(1)}, f32[16,4,512]{2,1,0:T(4,128)}, u32[]{:S(2)}) copy-start(f32[16,4,512]{2,1,0:T(4,128)} %est.1) | copy-start | bytes 393220
